TPU v7x, 32 devices: a whole 2x2x4 slice. The times are simulated.
32 devices in a mesh: win: 4 (over z), seq: 8 (over y, x, core).
Axes of the slice: x: 2, y: 2, z: 4, core: 2. Of those that a mesh axis runs over, the one named last changes fastest.
Arguments:
- layer_input: bfloat16 [8, 1024, 768], P('win', 'seq'), may hold values from -6 to 6
- d_out: bfloat16 [8, 1024, 768], P('win', 'seq'), may hold values from -13.5 to 13.5
- rand_ids: int32 [8, 16, 12, 3], P('win', 'seq'), may hold values from 0 to 15
- live_mask: int32 [8], P('win'), may hold values 0 or 1
- w_qkv: float32 [768, 2304], P('seq', 'win'), may hold values from -0.21875 to 0.21875
- w_out: float32 [768, 768], P('seq', 'win'), may hold values from -0.875 to 0.875
- w_up: float32 [768, 3072], P('seq', 'win'), may hold values from -0.25259074 to 0.25259074
- w_down: float32 [3072, 768], P('seq', 'win'), may hold values from -0.109375 to 0.109375
- norm_params: float32 [3072], P(('win', 'seq')), may hold values from -1.2 to 2, as said below
- m_qkv: float32 [768, 2304], P('seq', 'win'), may hold values from -0.0015031901 to 0.0015031901, as said below
- m_out: float32 [768, 768], P('seq', 'win'), may hold values from -0.0015031901 to 0.0015031901, as said below
- m_up: float32 [768, 3072], P('seq', 'win'), may hold values from -0.0015031901 to 0.0015031901, as said below
- m_down: float32 [3072, 768], P('seq', 'win'), may hold values from -0.0015031901 to 0.0015031901, as said below
- m_norm: float32 [3072], P(('win', 'seq')), may hold values from -0.0060127606 to 0.0060127606, as said below
- v_qkv: float32 [768, 2304], P('seq', 'win'), may hold values from 1.412238e-07 to 5.648952e-07
- v_out: float32 [768, 768], P('seq', 'win'), may hold values from 1.412238e-07 to 5.648952e-07
- v_up: float32 [768, 3072], P('seq', 'win'), may hold values from 1.412238e-07 to 5.648952e-07
- v_down: float32 [3072, 768], P('seq', 'win'), may hold values from 1.412238e-07 to 5.648952e-07
- v_norm: float32 [3072], P(('win', 'seq')), may hold values from 2.2595806e-06 to 9.0383225e-06
Outputs:
- output: bfloat16 [8, 1024, 768], P('win', 'seq')
- d_input: float32 [8, 1024, 768], P('win', 'seq')
- g_qkv: float32 [768, 2304], P('seq', 'win')
- g_out: float32 [768, 768], P('seq', 'win')
- g_up: float32 [768, 3072], P('seq', 'win')
- g_down: float32 [3072, 768], P('seq', 'win')
- g_norm: float32 [3072], P(('win', 'seq'))
- new_qkv: float32 [768, 2304], P('seq', 'win')
- new_out: float32 [768, 768], P('seq', 'win')
- new_up: float32 [768, 3072], P('seq', 'win')
- new_down: float32 [3072, 768], P('seq', 'win')
- new_norm: float32 [3072], P(('win', 'seq'))
- mom_qkv: float32 [768, 2304], P('seq', 'win')
- mom_out: float32 [768, 768], P('seq', 'win')
- mom_up: float32 [768, 3072], P('seq', 'win')
- mom_down: float32 [3072, 768], P('seq', 'win')
- mom_norm: float32 [3072], P(('win', 'seq'))
- sec_qkv: float32 [768, 2304], P('seq', 'win')
- sec_out: float32 [768, 768], P('seq', 'win')
- sec_up: float32 [768, 3072], P('seq', 'win')
- sec_down: float32 [3072, 768], P('seq', 'win')
- sec_norm: float32 [3072], P(('win', 'seq'))
- grad_norm: float32 [1], replicated
Inputs may be any that keep to these rules, and one draw needn't show every extreme that they name: `norm_params`: gains about 1 in the first and third pieces, shifts of both signs in the second and fourth. `m_qkv`: of both signs. `m_out`: of both signs. `m_up`: of both signs. `m_down`: of both signs. `m_norm`: of both signs.
All inputs are finite; a program needn't handle non-finite values. No bound on the sum of `live_mask` on one device may be relied on, other than what follows from the above.
Results may differ from a plain program's by a relative error of at most 0.035.
Values may be sent and summed in bfloat16 or wider, within the bound.
A program may use at most 320 MiB of HBM per device.

v0:
```python
import math

import jax
import jax.numpy as jnp
from jax import lax
from jax.sharding import PartitionSpec as P

H = 12
HD = 64
BLK = 64
STEP = 3


NEG = -1e30
ln_eps = 1e-05
beta_one = 0.5
beta_two = 0.5
adam_eps = 1e-08
decay_rate = 0.1
rate_matrix = 0.04
rate_output = 0.16
rate_norm = 0.6


def padded(block, sides, width):
    for axis, dim in sides:
        count = lax.axis_size(axis)
        forward = [(i, i + 1) for i in range(count - 1)]
        backward = [(target, source) for source, target in forward]
        low = lax.ppermute(
            lax.slice_in_dim(block, block.shape[dim] - width, None, axis=dim), axis, forward
        )
        high = lax.ppermute(lax.slice_in_dim(block, 0, width, axis=dim), axis, backward)
        block = jnp.concatenate([low, block, high], axis=dim)
    return block


def layer_norm(values, gain, shift):
    centre = values - jnp.mean(values, axis=-1, keepdims=True)
    spread = jnp.mean(centre * centre, axis=-1, keepdims=True)
    return centre * lax.rsqrt(spread + ln_eps) * gain + shift


def pick_slots(source, index):
    win_ix = jnp.arange(source.shape[0], dtype=jnp.int32)[:, None, None, None]
    head_ix = jnp.arange(source.shape[4], dtype=jnp.int32)[None, None, :, None]
    return source[win_ix, index, :, :, head_ix]


def adam_update(weight, grad, first, second, rate, decay, fix_one, fix_two):
    first_new = beta_one * first + (1.0 - beta_one) * grad
    second_new = beta_two * second + (1.0 - beta_two) * grad * grad
    stride = first_new / fix_one / (jnp.sqrt(second_new / fix_two) + adam_eps)
    return (weight - rate * (stride + decay * weight), first_new, second_new)


def per_device(
    layer_input,
    d_out,
    rand_ids,
    live_mask,
    w_qkv,
    w_out,
    w_up,
    w_down,
    norm_params,
    m_qkv,
    m_out,
    m_up,
    m_down,
    m_norm,
    v_qkv,
    v_out,
    v_up,
    v_down,
    v_norm,
):
    wins, local_len, width = layer_input.shape
    blocks_dev = local_len // BLK
    block_count = blocks_dev * lax.axis_size("seq")
    first_block = lax.axis_index("seq") * blocks_dev
    inv_root = 1.0 / math.sqrt(HD)
    rows = wins * local_len
    low_qkv = w_qkv.astype(jnp.bfloat16)
    low_out = w_out.astype(jnp.bfloat16)
    low_up = w_up.astype(jnp.bfloat16)
    low_down = w_down.astype(jnp.bfloat16)
    low_norm = norm_params.astype(jnp.bfloat16)
    rows_qkv, rows_out, rows_up, rows_down, rows_norm = (
        lax.all_gather(low_qkv, "seq", axis=0, tiled=True),
        lax.all_gather(low_out, "seq", axis=0, tiled=True),
        lax.all_gather(low_up, "seq", axis=0, tiled=True),
        lax.all_gather(low_down, "seq", axis=0, tiled=True),
        lax.all_gather(low_norm, "seq", axis=0, tiled=True),
    )
    full_qkv, full_out, full_up, full_down, full_norm = (
        lax.all_gather(rows_qkv, "win", axis=1, tiled=True),
        lax.all_gather(rows_out, "win", axis=1, tiled=True),
        lax.all_gather(rows_up, "win", axis=1, tiled=True),
        lax.all_gather(rows_down, "win", axis=1, tiled=True),
        lax.all_gather(rows_norm, "win", axis=0, tiled=True),
    )
    gains = full_norm.astype(jnp.float32).reshape(4, width)
    loss_weight = live_mask.astype(jnp.float32)
    here = first_block + jnp.arange(blocks_dev, dtype=jnp.int32)
    near_ids = jnp.stack(
        [jnp.maximum(here - 1, 0), here, jnp.minimum(here + 1, block_count - 1)], axis=1
    )
    near_ids = jnp.broadcast_to(near_ids[None, :, None, :], (wins, blocks_dev, H, 3))
    end_ids = jnp.broadcast_to(
        jnp.array([0, block_count - 1], dtype=jnp.int32), (wins, blocks_dev, H, 2)
    )
    far_ids = jnp.concatenate([end_ids, rand_ids], axis=3)
    all_ids = jnp.concatenate([near_ids, far_ids], axis=3)
    slot_count = all_ids.shape[3]
    valid = jnp.concatenate(
        [
            (here > 0)[:, None],
            jnp.ones((blocks_dev, 1), dtype=bool),
            (here < block_count - 1)[:, None],
            jnp.ones((blocks_dev, slot_count - 3), dtype=bool),
        ],
        axis=1,
    )
    key_valid = jnp.repeat(valid, BLK, axis=1)
    tokens = layer_input.astype(jnp.float32).reshape(rows, width)
    h_one = layer_norm(tokens, gains[0], gains[1]).astype(jnp.bfloat16)
    qkv = jnp.dot(h_one, full_qkv, preferred_element_type=jnp.float32)
    q_heads = (
        qkv[:, :width]
        .astype(jnp.bfloat16)
        .reshape(wins, blocks_dev, BLK, H, HD)
        .transpose(0, 1, 3, 2, 4)
    )
    keyval = qkv[:, width:].astype(jnp.bfloat16).reshape(wins, local_len, 2 * width)
    window = lax.all_gather(keyval, "seq", axis=1, tiled=True)
    shaped = window.reshape(wins, block_count, BLK, 2, H, HD)
    extended = padded(keyval, (("seq", 1),), BLK)
    shaped_ext = extended.reshape(wins, blocks_dev + 2, BLK, 2, H, HD)
    local_ids = (
        jnp.arange(blocks_dev, dtype=jnp.int32)[:, None] + jnp.arange(3, dtype=jnp.int32)[None, :]
    )
    local_ids = jnp.broadcast_to(local_ids[None, :, None, :], (wins, blocks_dev, H, 3))
    slots = jnp.concatenate(
        [pick_slots(shaped_ext, local_ids), pick_slots(shaped, far_ids)], axis=3
    )

    def split_slots(slot_data):
        keys = slot_data[:, :, :, :, :, 0, :].reshape(wins, blocks_dev, H, slot_count * BLK, HD)
        values = slot_data[:, :, :, :, :, 1, :].reshape(wins, blocks_dev, H, slot_count * BLK, HD)
        return (keys, values)

    def masked_scores(keys):
        raw = (
            jnp.einsum("wbhqd,wbhkd->wbhqk", q_heads, keys, preferred_element_type=jnp.float32)
            * inv_root
        )
        return jnp.where(key_valid[None, :, None, None, :], raw, NEG)

    keys, values = split_slots(slots)
    scores = masked_scores(keys)
    top = jnp.max(scores, axis=-1, keepdims=True)
    log_total = top + jnp.log(jnp.sum(jnp.exp(scores - top), axis=-1, keepdims=True))
    prob = jnp.exp(scores - log_total).astype(jnp.bfloat16)
    heads_out = jnp.einsum("wbhqk,wbhkd->wbhqd", prob, values, preferred_element_type=jnp.float32)
    attended = heads_out.astype(jnp.bfloat16).transpose(0, 1, 3, 2, 4).reshape(rows, width)
    middle = tokens + jnp.dot(attended, full_out, preferred_element_type=jnp.float32)
    h_two = layer_norm(middle, gains[2], gains[3]).astype(jnp.bfloat16)
    up_proj = jnp.dot(h_two, full_up, preferred_element_type=jnp.float32)
    active = jax.nn.gelu(up_proj).astype(jnp.bfloat16)
    result = middle + jnp.dot(active, full_down, preferred_element_type=jnp.float32)
    output = result.astype(jnp.bfloat16).reshape(wins, local_len, width)
    grad_y = (d_out.astype(jnp.float32) * loss_weight[:, None, None]).reshape(rows, width)
    grad_ffn = grad_y.astype(jnp.bfloat16)
    raw_down = jnp.einsum("tf,td->fd", active, grad_ffn, preferred_element_type=jnp.float32)
    grad_act = jnp.einsum("td,fd->tf", grad_ffn, full_down, preferred_element_type=jnp.float32)
    gelu_pull = jax.vjp(jax.nn.gelu, up_proj)[1]
    grad_up = gelu_pull(grad_act)[0].astype(jnp.bfloat16)
    raw_up = jnp.einsum("td,tf->df", h_two, grad_up, preferred_element_type=jnp.float32)
    grad_h_two = jnp.einsum("tf,df->td", grad_up, full_up, preferred_element_type=jnp.float32)
    norm_pull = jax.vjp(layer_norm, middle, gains[2], gains[3])[1]
    grad_mid_ln, raw_gain_two, raw_shift_two = norm_pull(grad_h_two)
    grad_mid = grad_y + grad_mid_ln
    grad_att = grad_mid.astype(jnp.bfloat16)
    raw_out = jnp.einsum("td,te->de", attended, grad_att, preferred_element_type=jnp.float32)
    grad_o = jnp.einsum("te,de->td", grad_att, full_out, preferred_element_type=jnp.float32)
    grad_o = (
        grad_o.astype(jnp.bfloat16).reshape(wins, blocks_dev, BLK, H, HD).transpose(0, 1, 3, 2, 4)
    )
    again = lax.all_gather(keyval, "seq", axis=1, tiled=True)
    back_keys, back_values = split_slots(
        pick_slots(again.reshape(wins, block_count, BLK, 2, H, HD), all_ids)
    )
    prob_f = jnp.exp(masked_scores(back_keys) - log_total)
    grad_p = jnp.einsum(
        "wbhqd,wbhkd->wbhqk", grad_o, back_values, preferred_element_type=jnp.float32
    )
    inner = jnp.sum(prob_f * grad_p, axis=-1, keepdims=True)
    grad_s = (prob_f * (grad_p - inner)).astype(jnp.bfloat16)
    grad_q = (
        jnp.einsum("wbhqk,wbhkd->wbhqd", grad_s, back_keys, preferred_element_type=jnp.float32)
        * inv_root
    )
    grad_v = jnp.einsum(
        "wbhqk,wbhqd->wbhkd",
        prob_f.astype(jnp.bfloat16),
        grad_o,
        preferred_element_type=jnp.float32,
    )
    grad_k = (
        jnp.einsum("wbhqk,wbhqd->wbhkd", grad_s, q_heads, preferred_element_type=jnp.float32)
        * inv_root
    )
    grad_slots = jnp.stack(
        [
            grad_k.reshape(wins, blocks_dev, H, slot_count, BLK, HD),
            grad_v.reshape(wins, blocks_dev, H, slot_count, BLK, HD),
        ],
        axis=5,
    )
    head_ix = jnp.arange(H, dtype=jnp.int32)[None, :, None]

    def send_back(items):
        index, slot_grads = items
        buffer = (
            jnp.zeros((block_count, BLK, 2, H, HD), jnp.float32)
            .at[index, :, :, head_ix]
            .add(slot_grads)
        )
        return lax.psum_scatter(
            buffer.reshape(block_count * BLK, 2 * width).astype(jnp.bfloat16),
            "seq",
            scatter_dimension=0,
            tiled=True,
        ).astype(jnp.float32)

    grad_kv = lax.map(send_back, (all_ids, grad_slots)).reshape(rows, 2 * width)
    grad_q_rows = grad_q.transpose(0, 1, 3, 2, 4).reshape(rows, width).astype(jnp.bfloat16)
    grad_qkv = jnp.concatenate([grad_q_rows, grad_kv.astype(jnp.bfloat16)], axis=1)
    raw_qkv = jnp.einsum("td,te->de", h_one, grad_qkv, preferred_element_type=jnp.float32)
    grad_h_one = jnp.einsum("te,de->td", grad_qkv, full_qkv, preferred_element_type=jnp.float32)
    first_pull = jax.vjp(layer_norm, tokens, gains[0], gains[1])[1]
    grad_tok_ln, raw_gain_one, raw_shift_one = first_pull(grad_h_one)
    d_input = (grad_mid + grad_tok_ln).reshape(wins, local_len, width)
    raw_norm = jnp.concatenate([raw_gain_one, raw_shift_one, raw_gain_two, raw_shift_two])
    part_qkv, part_out, part_up, part_down, part_norm = (
        lax.psum_scatter(
            raw_qkv.astype(jnp.bfloat16), "win", scatter_dimension=1, tiled=True
        ).astype(jnp.float32),
        lax.psum_scatter(
            raw_out.astype(jnp.bfloat16), "win", scatter_dimension=1, tiled=True
        ).astype(jnp.float32),
        lax.psum_scatter(
            raw_up.astype(jnp.bfloat16), "win", scatter_dimension=1, tiled=True
        ).astype(jnp.float32),
        lax.psum_scatter(
            raw_down.astype(jnp.bfloat16), "win", scatter_dimension=1, tiled=True
        ).astype(jnp.float32),
        lax.psum_scatter(
            raw_norm.astype(jnp.bfloat16), "win", scatter_dimension=0, tiled=True
        ).astype(jnp.float32),
    )
    red_qkv, red_out, red_up, red_down, red_norm = (
        lax.psum_scatter(
            part_qkv.astype(jnp.bfloat16), "seq", scatter_dimension=0, tiled=True
        ).astype(jnp.float32),
        lax.psum_scatter(
            part_out.astype(jnp.bfloat16), "seq", scatter_dimension=0, tiled=True
        ).astype(jnp.float32),
        lax.psum_scatter(
            part_up.astype(jnp.bfloat16), "seq", scatter_dimension=0, tiled=True
        ).astype(jnp.float32),
        lax.psum_scatter(
            part_down.astype(jnp.bfloat16), "seq", scatter_dimension=0, tiled=True
        ).astype(jnp.float32),
        lax.psum_scatter(
            part_norm.astype(jnp.bfloat16), "seq", scatter_dimension=0, tiled=True
        ).astype(jnp.float32),
    )
    reduced = (red_qkv, red_out, red_up, red_down, red_norm)
    local_squares = jnp.float32(0.0)
    for grad in reduced:
        local_squares = local_squares + jnp.sum(grad * grad)
    grad_norm = jnp.sqrt(lax.psum(local_squares, ("win", "seq")))
    factor = 1.0 / jnp.maximum(grad_norm, 1.0)
    clipped = tuple((grad * factor for grad in reduced))
    count = jnp.float32(STEP)
    fix_one = 1.0 - jnp.power(jnp.float32(beta_one), count)
    fix_two = 1.0 - jnp.power(jnp.float32(beta_two), count)
    params = (w_qkv, w_out, w_up, w_down, norm_params)
    firsts = (m_qkv, m_out, m_up, m_down, m_norm)
    seconds = (v_qkv, v_out, v_up, v_down, v_norm)
    rates = (rate_matrix, rate_output, rate_matrix, rate_matrix, rate_norm)
    news, moms, secs = ([], [], [])
    for index in range(5):
        decay = 0.0 if index == 4 else decay_rate
        new_w, new_m, new_v = adam_update(
            params[index],
            clipped[index],
            firsts[index],
            seconds[index],
            rates[index],
            decay,
            fix_one,
            fix_two,
        )
        news.append(new_w)
        moms.append(new_m)
        secs.append(new_v)
    return (
        output,
        d_input,
        clipped[0],
        clipped[1],
        clipped[2],
        clipped[3],
        clipped[4],
        news[0],
        news[1],
        news[2],
        news[3],
        news[4],
        moms[0],
        moms[1],
        moms[2],
        moms[3],
        moms[4],
        secs[0],
        secs[1],
        secs[2],
        secs[3],
        secs[4],
        grad_norm.reshape(1),
    )


def solution(mesh):
    placed = (
        P("win", "seq", None),
        P("win", "seq", None),
        P("win", "seq", None, None),
        P("win"),
        P("seq", "win"),
        P("seq", "win"),
        P("seq", "win"),
        P("seq", "win"),
        P(("win", "seq")),
        P("seq", "win"),
        P("seq", "win"),
        P("seq", "win"),
        P("seq", "win"),
        P(("win", "seq")),
        P("seq", "win"),
        P("seq", "win"),
        P("seq", "win"),
        P("seq", "win"),
        P(("win", "seq")),
    )
    return jax.shard_map(
        per_device,
        mesh=mesh,
        in_specs=placed,
        out_specs=(
            P("win", "seq", None),
            P("win", "seq", None),
            P("seq", "win"),
            P("seq", "win"),
            P("seq", "win"),
            P("seq", "win"),
            P(("win", "seq")),
            P("seq", "win"),
            P("seq", "win"),
            P("seq", "win"),
            P("seq", "win"),
            P(("win", "seq")),
            P("seq", "win"),
            P("seq", "win"),
            P("seq", "win"),
            P("seq", "win"),
            P(("win", "seq")),
            P("seq", "win"),
            P("seq", "win"),
            P("seq", "win"),
            P("seq", "win"),
            P(("win", "seq")),
            P(),
        ),
        check_vma=False,
    )
```

profile of v0, /device:TPU:0, one launch (start us, length us, event | category | flops | bytes accessed | tf_op | source)
XLA Modules:
  0.0 1226.2 jit_solution(14075395186851476843)
XLA Ops:
  10.0 12.3 %all_gather.36 = bf16[768,576]{1,0:T(8,128)(2,1)S(1)} all-gather(bf16[96,576]{1,0:T(8,128)(2,1)S(1)} %convert_element_type.133), channel_id=1, replica_groups=mesh['win'=4,'seq'=8] {'seq'}, dimensions={0}, use_global_device_ids=true | all-gather | bytes 995328 | tf_op jit(solution)/shard_map/all_gather | solution.py:90
  24.4 13.0 %all-gather.19.cloned.1.call-done = bf16[3072,192]{0,1:T(8,128)(2,1)} async-done(((bf16[384,192]{0,1:T(8,128)(2,1)}), bf16[3072,192]{0,1:T(8,128)(2,1)}) %all-gather.19.cloned.1.call-update) | async-done | bytes 1179664 | tf_op jit(solution)/shard_map/all_gather | solution.py:93
  39.0 13.1 %all-reduce = bf16[768]{0:T(1024)(128)(2,1)S(1)} all-reduce(bf16[768]{0:T(1024)(128)(2,1)S(1)} %dynamic-update-slice), channel_id=1, replica_groups=mesh['win'=4,'seq'=8] {'seq'}, use_global_device_ids=true, to_apply=%add | all-reduce | flops 768 | bytes 3072
  52.1 13.3 %all-gather = bf16[4,1,768]{2,1,0:T(2,128)(2,1)S(1)} all-gather(bf16[1,1,768]{2,1,0:T(2,128)(2,1)S(1)} %reshape.467), channel_id=1, replica_groups=mesh['win'=4,'seq'=8] {'win'}, dimensions={0}, use_global_device_ids=true | all-gather | bytes 7680 | tf_op jit(solution)/shard_map/all_gather | solution.py:101
  66.8 42.3 %all-gather.9.cloned.1.call-done = bf16[768,2304]{0,1:T(8,128)(2,1)} async-done(((bf16[768,576]{0,1:T(8,128)(2,1)}), bf16[768,2304]{0,1:T(8,128)(2,1)}) %all-gather.9.cloned.1.call-update) | async-done | bytes 3538960 | tf_op jit(solution)/shard_map/all_gather | solution.py:97
  155.2 14.6 %gather_fusion = bf16[144,64,2,64]{3,1,2,0:T(8,128)(2,1)} fusion(bf16[2,4,64,2,12,64]{5,2,4,3,1,0:T(8,128)(2,1)S(1)} %copy.203, s32[144]{0:T(256)S(1)} %reshape.439), kind=kCustom, calls=%fused_computation | custom fusion | bytes 4720320 | tf_op jit(solution)/shard_map/gather | solution.py:47
  169.8 55.5 %all-gather.21.cloned.1.call-done = bf16[3072,768]{0,1:T(8,128)(2,1)} async-done(((bf16[3072,192]{0,1:T(8,128)(2,1)}), bf16[3072,768]{0,1:T(8,128)(2,1)}) %all-gather.21.cloned.1.call-update) | async-done | bytes 4718608 | tf_op jit(solution)/shard_map/all_gather | solution.py:100
  230.8 40.8 %all-gather.11.cloned.1.call-done = bf16[2,1024,1536]{2,1,0:T(8,128)(2,1)} async-done(((bf16[2,128,1536]{2,1,0:T(8,128)(2,1)}), bf16[2,1024,1536]{2,1,0:T(8,128)(2,1)}) %all-gather.11.cloned.1.call-update) | async-done | bytes 6291472 | tf_op jit(solution)/shard_map/all_gather | solution.py:136
  271.6 21.0 %reshape.495 = bf16[2,16,64,2,12,64]{5,4,3,2,1,0:T(8,128)(2,1)} reshape(bf16[2,1024,1536]{2,1,0:T(8,128)(2,1)} %all-gather.11.cloned.1.call-done) | data formatting | bytes 12582912 | tf_op jit(solution)/shard_map/reshape | solution.py:137
  292.5 12.2 copy.206
  304.8 19.5 %gather_fusion.1 = bf16[240,64,2,64]{3,1,2,0:T(8,128)(2,1)} fusion(bf16[2,16,64,2,12,64]{5,2,4,3,1,0:T(8,128)(2,1)} %copy.206, s32[240]{0:T(256)S(1)} %reshape.445), kind=kCustom, calls=%fused_computation.1 | custom fusion | bytes 7867200 | tf_op jit(solution)/shard_map/gather | solution.py:47
  324.3 22.6 %gather_fusion.2 = bf16[384,64,2,64]{3,1,2,0:T(8,128)(2,1)} fusion(bf16[2,16,64,2,12,64]{5,2,4,3,1,0:T(8,128)(2,1)} %copy.206, s32[384]{0:T(512)S(1)} %reshape.451), kind=kCustom, calls=%fused_computation.2 | custom fusion | bytes 12587520 | tf_op jit(solution)/shard_map/gather | solution.py:47
  362.6 12.6 %fusion.81 = (bf16[2,2,12,8,64,1,64]{6,4,5,3,2,1,0:T(8,128)(2,1)}, bf16[2,2,12,8,64,1,64]{6,4,5,3,2,1,0:T(8,128)(2,1)}) fusion(bf16[2,2,12,8,64,2,64]{6,4,5,3,2,1,0:T(8,128)(2,1)} %bitcast.116), kind=kLoop, calls=%fused_computation.180 | loop fusion | bytes 12582912 | tf_op jit(solution)/shard_map/slice | solution.py:150
  375.2 19.0 %all-gather.17.cloned.1.call-done = bf16[768,3072]{1,0:T(8,128)(2,1)} async-done(((bf16[768,768]{1,0:T(8,128)(2,1)}), bf16[768,3072]{1,0:T(8,128)(2,1)}) %all-gather.17.cloned.1.call-update) | async-done | bytes 4718608 | tf_op jit(solution)/shard_map/all_gather | solution.py:99
  440.2 18.5 %pad_maximum_fusion = f32[2,2,12,8,64,2,64]{6,4,5,3,2,1,0:T(8,128)} fusion(f32[2,2,12,8,64,1,64]{6,4,5,3,2,1,0:T(8,128)} %bitcast.118, f32[2,2,12,8,64,1,64]{6,4,5,3,2,1,0:T(8,128)} %bitcast.117), kind=kLoop, calls=%fused_computation.17 | loop fusion | flops 3145728 | bytes 25165824 | tf_op jit(solution)/shard_map/stack | solution.py:214
  458.7 267.2 %while.11 = (s32[]{:T(128)}, bf16[2,128,1536]{2,1,0:T(8,128)(2,1)}, s32[2,2,12,8]{3,2,1,0:T(8,128)S(1)}, f32[2,2,12,8,64,2,64]{6,4,5,3,2,1,0:T(8,128)}, s32[]{:T(128)}, /*index=5*/f32[]{:T(128)}) while((s32[]{:T(128)}, bf16[2,128,1536]{2,1,0:T(8,128)(2,1)}, s32[2,2,12,8]{3,2,1,0:T(8,128)S(1)}, ...), condition=%wide.region_12.13_spmd.clone, body=%wide.region_9.12_spmd.clone.sunk | while | flops 3147506 | bytes 79041328 | solution.py:237
  459.3 11.8 constant_dynamic-slice_fusion.2
  477.3 40.5 %scatter_fusion = f32[16,64,2,12,64]{4,1,3,2,0:T(8,128)} fusion(f32[16,64,2,12,64]{4,1,3,2,0:T(8,128)} %broadcast.646, s32[192]{0:T(256)S(1)} %reshape.509, f32[192,64,2,64]{3,1,2,0:T(8,128)} %bitcast.113), kind=kCustom, calls=%fused_computation.3.clone.clone.1 | custom fusion | flops 1572864 | bytes 18875904 | tf_op jit(solution)/shard_map/while/body/eval_jaxpr/scatter-add | solution.py:228
  532.6 11.4 reshape.510
  544.1 45.2 %reduce-scatter.36.cloned.1.call-done = bf16[128,1536]{1,0:T(8,128)(2,1)} async-done(((bf16[1024,1536]{1,0:T(8,128)(2,1)}), bf16[128,1536]{1,0:T(8,128)(2,1)}) %reduce-scatter.36.cloned.1.call-update) | async-done | bytes 393232 | tf_op jit(solution)/shard_map/while
  591.9 11.8 constant_dynamic-slice_fusion.2
  609.9 40.4 %scatter_fusion = f32[16,64,2,12,64]{4,1,3,2,0:T(8,128)} fusion(f32[16,64,2,12,64]{4,1,3,2,0:T(8,128)} %broadcast.646, s32[192]{0:T(256)S(1)} %reshape.509, f32[192,64,2,64]{3,1,2,0:T(8,128)} %bitcast.113), kind=kCustom, calls=%fused_computation.3.clone.clone.1 | custom fusion | flops 1572864 | bytes 18875904 | tf_op jit(solution)/shard_map/while/body/eval_jaxpr/scatter-add | solution.py:228
  665.1 11.4 reshape.510
  676.5 46.8 %reduce-scatter.36.cloned.1.call-done = bf16[128,1536]{1,0:T(8,128)(2,1)} async-done(((bf16[1024,1536]{1,0:T(8,128)(2,1)}), bf16[128,1536]{1,0:T(8,128)(2,1)}) %reduce-scatter.36.cloned.1.call-update) | async-done | bytes 393232 | tf_op jit(solution)/shard_map/while
  759.9 65.5 %reduce-scatter.20.cloned.1.call-done = bf16[768,576]{0,1:T(8,128)(2,1)} async-done(((bf16[768,2304]{0,1:T(8,128)(2,1)}), bf16[768,576]{0,1:T(8,128)(2,1)}) %reduce-scatter.20.cloned.1.call-update) | async-done | bytes 884752 | tf_op jit(solution)/shard_map/reduce_scatter | solution.py:247
  827.7 85.4 %reduce-scatter.28.cloned.1.call-done = bf16[3072,192]{0,1:T(8,128)(2,1)} async-done(((bf16[3072,768]{0,1:T(8,128)(2,1)}), bf16[3072,192]{0,1:T(8,128)(2,1)}) %reduce-scatter.28.cloned.1.call-update) | async-done | bytes 1179664 | tf_op jit(solution)/shard_map/reduce_scatter | solution.py:256
  924.7 76.5 %reduce-scatter.24.cloned.1.call-done = bf16[768,768]{1,0:T(8,128)(2,1)} async-done(((bf16[768,3072]{1,0:T(8,128)(2,1)}), bf16[768,768]{1,0:T(8,128)(2,1)}) %reduce-scatter.24.cloned.1.call-update) | async-done | bytes 1179664 | tf_op jit(solution)/shard_map/reduce_scatter | solution.py:253
  1012.9 12.1 all-reduce.2
  1040.6 37.3 %reduce-scatter.30.cloned.1.call-done = bf16[96,576]{1,0:T(8,128)(2,1)} async-done(((bf16[768,576]{1,0:T(8,128)(2,1)}), bf16[96,576]{1,0:T(8,128)(2,1)}) %reduce-scatter.30.cloned.1.call-update) | async-done | bytes 110608
  1081.0 38.9 %reduce-scatter.34.cloned.1.call-done = bf16[384,192]{1,0:T(8,128)(2,1)} async-done(((bf16[3072,192]{1,0:T(8,128)(2,1)}), bf16[384,192]{1,0:T(8,128)(2,1)}) %reduce-scatter.34.cloned.1.call-update) | async-done | bytes 147472
  1121.7 38.5 %reduce-scatter.26.cloned.1.call-done = bf16[96,768]{1,0:T(8,128)(2,1)} async-done(((bf16[768,768]{1,0:T(8,128)(2,1)}), bf16[96,768]{1,0:T(8,128)(2,1)}) %reduce-scatter.26.cloned.1.call-update) | async-done | bytes 147472 | tf_op jit(solution)/shard_map/reduce_scatter | solution.py:270
  1164.9 39.3 %psum.7 = f32[]{:T(128)} all-reduce(f32[]{:T(128)S(6)} %add.335), channel_id=1, replica_groups=mesh['win'=4,'seq'=8] {'win','seq'}, use_global_device_ids=true, to_apply=%region_34.35 | all-reduce | flops 1 | bytes 8 | tf_op jit(solution)/shard_map/psum | solution.py:284
  (340 shorter events, 260.4 us)
Async XLA Ops:
  7.2 30.2 %all-gather.19.cloned.1.call-start = ((), (), s32[]{:S(2)}) async-start(), calls=%async_computation.14 | async-start | bytes 1327104 | tf_op jit(solution)/shard_map/all_gather | solution.py:93
  9.0 100.1 %all-gather.9.cloned.1.call-start = ((), (), s32[]{:S(2)}) async-start(), calls=%async_computation.9 | async-start | bytes 4423680 | tf_op jit(solution)/shard_map/all_gather | solution.py:97
  23.6 110.8 %all-gather.15.cloned.1.call-start = ((), (), s32[]{:S(2)}) async-start(), calls=%async_computation.12 | async-start | bytes 1327104 | tf_op jit(solution)/shard_map/all_gather | solution.py:92
  24.4 200.9 %all-gather.21.cloned.1.call-start = ((), (), s32[]{:S(2)}) async-start(), calls=%async_computation.15 | async-start | bytes 5898240 | tf_op jit(solution)/shard_map/all_gather | solution.py:100
  37.4 234.1 %all-gather.11.cloned.1.call-start = ((), (), s32[]{:S(2)}) async-start(), calls=%async_computation.10 | async-start | bytes 7077888 | tf_op jit(solution)/shard_map/all_gather | solution.py:136
  113.2 247.1 %all-gather.13.cloned.1.call-start = ((), (), s32[]{:S(2)}) async-start(), calls=%async_computation.11 | async-start | bytes 1474560 | tf_op jit(solution)/shard_map/all_gather | solution.py:98
  124.3 269.8 %all-gather.17.cloned.1.call-start = ((), (), s32[]{:S(2)}) async-start(), calls=%async_computation.13 | async-start | bytes 5898240 | tf_op jit(solution)/shard_map/all_gather | solution.py:99
  136.7 9.0 collective-permute-start
  139.6 6.1 collective-permute-start.1
  459.1 130.2 %reduce-scatter.36.cloned.1.call-start = ((), (), s32[]{:S(2)}) async-start(), calls=%async_computation.24 | async-start | bytes 3538944 | tf_op jit(solution)/shard_map/while
  591.7 131.6 %reduce-scatter.36.cloned.1.call-start = ((), (), s32[]{:S(2)}) async-start(), calls=%async_computation.24 | async-start | bytes 3538944 | tf_op jit(solution)/shard_map/while
  725.9 32.0 %reduce-scatter.22.cloned.1.call-start = ((), (), s32[]{:S(2)}) async-start(), calls=%async_computation.17 | async-start | bytes 1474560 | tf_op jit(solution)/shard_map/reduce_scatter | solution.py:250
  726.5 98.9 %reduce-scatter.20.cloned.1.call-start = ((), (), s32[]{:S(2)}) async-start(), calls=%async_computation.16 | async-start | bytes 4423680 | tf_op jit(solution)/shard_map/reduce_scatter | solution.py:247
  735.8 177.2 %reduce-scatter.28.cloned.1.call-start = ((), (), s32[]{:S(2)}) async-start(), calls=%async_computation.20 | async-start | bytes 5898240 | tf_op jit(solution)/shard_map/reduce_scatter | solution.py:256
  741.6 259.6 %reduce-scatter.24.cloned.1.call-start = ((), (), s32[]{:S(2)}) async-start(), calls=%async_computation.18 | async-start | bytes 5898240 | tf_op jit(solution)/shard_map/reduce_scatter | solution.py:253
  747.0 168.7 %copy-start.32 = (f32[96,192]{1,0:T(8,128)S(1)}, f32[96,192]{1,0:T(8,128)}, u32[]{:S(2)}) copy-start(f32[96,192]{1,0:T(8,128)} %param.27) | copy-start | bytes 221188
  747.0 168.8 %copy-start.23 = (f32[96,576]{1,0:T(8,128)S(1)}, f32[96,576]{1,0:T(8,128)}, u32[]{:S(2)}) copy-start(f32[96,576]{1,0:T(8,128)} %param.26) | copy-start | bytes 663556
  747.0 169.0 %copy-start.67 = (u32[32]{0:T(128)S(1)}, u32[32]{0:T(128)}, u32[]{:S(2)}) copy-start(u32[32]{0:T(128)} %constant.225) | copy-start | bytes 388
  747.0 169.5 %copy-start.42 = (f32[96,192]{1,0:T(8,128)S(1)}, f32[96,192]{1,0:T(8,128)}, u32[]{:S(2)}) copy-start(f32[96,192]{1,0:T(8,128)} %param.32) | copy-start | bytes 221188
  747.0 170.3 %copy-start.43 = (f32[96,192]{1,0:T(8,128)S(1)}, f32[96,192]{1,0:T(8,128)}, u32[]{:S(2)}) copy-start(f32[96,192]{1,0:T(8,128)} %param.37) | copy-start | bytes 221188
  747.0 171.0 %copy-start.36 = (f32[96,576]{1,0:T(8,128)S(1)}, f32[96,576]{1,0:T(8,128)}, u32[]{:S(2)}) copy-start(f32[96,576]{1,0:T(8,128)} %param.31) | copy-start | bytes 663556
  747.1 292.0 %reduce-scatter.32.cloned.1.call-start = ((), (), s32[]{:S(2)}) async-start(), calls=%async_computation.22 | async-start | bytes 442368
  759.8 158.4 %copy-start.37 = (f32[96,576]{1,0:T(8,128)S(1)}, f32[96,576]{1,0:T(8,128)}, u32[]{:S(2)}) copy-start(f32[96,576]{1,0:T(8,128)} %param.36) | copy-start | bytes 663556
  759.8 160.6 %copy-start.4 = (bf16[2,128,768]{2,1,0:T(8,128)(2,1)S(1)}, bf16[2,128,768]{2,1,0:T(8,128)(2,1)}, u32[]{:S(2)}) copy-start(bf16[2,128,768]{2,1,0:T(8,128)(2,1)} %param.22) | copy-start | bytes 1179652
  759.8 160.6 %copy-start.45 = (f32[768]{0:T(1024)S(1)}, f32[768]{0:T(1024)}, u32[]{:S(2)}) copy-start(f32[768]{0:T(1024)} %copy-done.44) | copy-start | bytes 9220
  759.8 160.6 %copy-start.50 = (f32[256]{0:T(256)S(1)}, f32[256]{0:T(256)}, u32[]{:S(2)}) copy-start(f32[256]{0:T(256)} %copy-done.49) | copy-start | bytes 3076
  759.9 318.1 %reduce-scatter.30.cloned.1.call-start = ((), (), s32[]{:S(2)}) async-start(), calls=%async_computation.21 | async-start | bytes 1105920
  827.6 292.3 %reduce-scatter.34.cloned.1.call-start = ((), (), s32[]{:S(2)}) async-start(), calls=%async_computation.23 | async-start | bytes 1769472
  915.7 244.5 %reduce-scatter.26.cloned.1.call-start = ((), (), s32[]{:S(2)}) async-start(), calls=%async_computation.19 | async-start | bytes 1327104 | tf_op jit(solution)/shard_map/reduce_scatter | solution.py:270
  1025.7 138.0 %copy-start.7 = (f32[256,768]{1,0:T(8,128)S(1)}, f32[256,768]{1,0:T(8,128)}, u32[]{:S(2)}) copy-start(f32[256,768]{1,0:T(8,128)} %copy-done.6) | copy-start | bytes 2359300
  1079.0 134.5 %copy-start.62 = (f32[96]{0:T(128)S(1)}, f32[96]{0:T(128)}, u32[]{:S(2)}) copy-start(f32[96]{0:T(128)} %param.30) | copy-start | bytes 1156
  1079.0 135.1 %copy-start.20 = (f32[384,192]{0,1:T(8,128)S(1)}, f32[384,192]{0,1:T(8,128)}, u32[]{:S(2)}) copy-start(f32[384,192]{0,1:T(8,128)} %param.29) | copy-start | bytes 884740
  (59 other events, 1744.8 us)
Sparse Core Ops, SparseCore 0:
  10.5 26.8 all-gather.18
  39.0 70.0 all-gather.8
  111.6 22.7 all-gather.14
  135.8 89.3 all-gather.20
  227.6 43.9 all-gather.10
  273.6 30.4 all-gather.12
  305.6 88.5 all-gather.16
  544.2 45.0 reduce-scatter.35
  676.7 46.6 reduce-scatter.35
  728.7 29.1 reduce-scatter.21
  760.2 65.0 reduce-scatter.19
  827.5 85.5 reduce-scatter.27
  915.4 85.7 reduce-scatter.23
  1004.7 34.3 reduce-scatter.31
  1042.1 35.7 reduce-scatter.29
  1081.4 38.4 reduce-scatter.33
  1123.3 36.7 reduce-scatter.25
where the time goes:
time: 1230 us
  waiting for transfers between devices  631 us (51%)
  local copies, waits for them, and re-layouts  238 us (19%)
  other arithmetic  145 us (12%)
  blocking collectives  111 us (9%)
  matrix products  73.7 us (6%)
  between operations  22.4 us (2%)
    while x4, waiting for transfers between devices  92 us
    reduce_scatter x1, waiting for transfers between devices, per_device(): lax.psum_scatter(raw_down.astype(jnp.bfloat16), 'win', scatter_dimension=...  85.4 us
    unnamed x18, waiting for transfers between devices  84.3 us
    scatter-add x2, other arithmetic, send_back(): buffer = jnp.zeros((block_count, BLK, 2, H, HD), jnp.float32).at[index, :...  80.8 us
    reduce_scatter x1, waiting for transfers between devices, per_device(): lax.psum_scatter(raw_up.astype(jnp.bfloat16), 'win', scatter_dimension=1,...  76.5 us
    reduce_scatter x1, waiting for transfers between devices, per_device(): lax.psum_scatter(raw_qkv.astype(jnp.bfloat16), 'win', scatter_dimension=1...  65.5 us
    gather x3, local copies, waits for them, and re-layouts, pick_slots(): return source[win_ix, index, :, :, head_ix]  56.6 us
    all_gather x1, waiting for transfers between devices, per_device(): lax.all_gather(rows_down, 'win', axis=1, tiled=True)  55.5 us
  transfers between devices with their start and end apart: 19, of which 16 were waited for; matrix products, arithmetic and copies ran while one was open for 16% of the time, Pallas kernels for 0%

commit v1 on v0

v1 whole, which is shorter than its diff:
```python
import math

import jax
import jax.numpy as jnp
from jax import lax
from jax.sharding import PartitionSpec as P

H = 12
HD = 64
BLK = 64
STEP = 3


NEG = -1e30
ln_eps = 1e-05
beta_one = 0.5
beta_two = 0.5
adam_eps = 1e-08
decay_rate = 0.1
rate_matrix = 0.04
rate_output = 0.16
rate_norm = 0.6


def layer_norm(values, gain, shift):
    centre = values - jnp.mean(values, axis=-1, keepdims=True)
    spread = jnp.mean(centre * centre, axis=-1, keepdims=True)
    return centre * lax.rsqrt(spread + ln_eps) * gain + shift


def slot_counts(rand_ids, first_block, block_count):
    blocks_dev = rand_ids.shape[1]
    here = (first_block + jnp.arange(blocks_dev, dtype=jnp.int32))[:, None]
    every = jnp.arange(block_count, dtype=jnp.int32)[None, :]
    near = (jnp.abs(here - every) <= 1).astype(jnp.float32)
    ends = (every == 0).astype(jnp.float32) + (every == block_count - 1).astype(jnp.float32)
    drawn = jnp.sum((rand_ids[..., None] == every[0]).astype(jnp.float32), axis=3)
    return (near + ends)[None, :, None, :] + drawn


def adam_update(weight, grad, first, second, rate, decay, fix_one, fix_two):
    first_new = beta_one * first + (1.0 - beta_one) * grad
    second_new = beta_two * second + (1.0 - beta_two) * grad * grad
    stride = first_new / fix_one / (jnp.sqrt(second_new / fix_two) + adam_eps)
    return (weight - rate * (stride + decay * weight), first_new, second_new)


def per_device(
    layer_input,
    d_out,
    rand_ids,
    live_mask,
    w_qkv,
    w_out,
    w_up,
    w_down,
    norm_params,
    m_qkv,
    m_out,
    m_up,
    m_down,
    m_norm,
    v_qkv,
    v_out,
    v_up,
    v_down,
    v_norm,
):
    wins, local_len, width = layer_input.shape
    blocks_dev = local_len // BLK
    block_count = blocks_dev * lax.axis_size("seq")
    first_block = lax.axis_index("seq") * blocks_dev
    inv_root = 1.0 / math.sqrt(HD)
    rows = wins * local_len
    low_qkv = w_qkv.astype(jnp.bfloat16)
    low_out = w_out.astype(jnp.bfloat16)
    low_up = w_up.astype(jnp.bfloat16)
    low_down = w_down.astype(jnp.bfloat16)
    low_norm = norm_params.astype(jnp.bfloat16)
    full_qkv, full_out, full_up, full_down = (
        lax.all_gather(lax.all_gather(low, "win", axis=1, tiled=True), "seq", axis=0, tiled=True)
        for low in (low_qkv, low_out, low_up, low_down)
    )
    full_norm = lax.all_gather(low_norm, ("win", "seq"), axis=0, tiled=True)
    gains = full_norm.astype(jnp.float32).reshape(4, width)
    loss_weight = live_mask.astype(jnp.float32)
    counts = slot_counts(rand_ids, first_block, block_count)
    bias = jnp.where(counts > 0, jnp.log(jnp.maximum(counts, 1.0)), NEG)
    bias = jnp.repeat(bias, BLK, axis=3)[:, :, :, None, :]
    tokens = layer_input.astype(jnp.float32).reshape(rows, width)
    h_one = layer_norm(tokens, gains[0], gains[1]).astype(jnp.bfloat16)
    qkv = jnp.dot(h_one, full_qkv, preferred_element_type=jnp.float32)
    q_heads = qkv[:, :width].astype(jnp.bfloat16).reshape(wins, blocks_dev, BLK, H, HD)
    keyval = qkv[:, width:].astype(jnp.bfloat16).reshape(wins, local_len, 2 * width)
    window = lax.all_gather(keyval, "seq", axis=1, tiled=True)
    shaped = window.reshape(wins, block_count * BLK, 2, H, HD)
    keys, values = shaped[:, :, 0], shaped[:, :, 1]
    scores = (
        jnp.einsum("wbqhd,wkhd->wbhqk", q_heads, keys, preferred_element_type=jnp.float32)
        * inv_root
        + bias
    )
    top = jnp.max(scores, axis=-1, keepdims=True)
    log_total = top + jnp.log(jnp.sum(jnp.exp(scores - top), axis=-1, keepdims=True))
    prob = jnp.exp(scores - log_total).astype(jnp.bfloat16)
    heads_out = jnp.einsum("wbhqk,wkhd->wbqhd", prob, values, preferred_element_type=jnp.float32)
    attended = heads_out.astype(jnp.bfloat16).reshape(rows, width)
    middle = tokens + jnp.dot(attended, full_out, preferred_element_type=jnp.float32)
    h_two = layer_norm(middle, gains[2], gains[3]).astype(jnp.bfloat16)
    up_proj = jnp.dot(h_two, full_up, preferred_element_type=jnp.float32)
    active = jax.nn.gelu(up_proj).astype(jnp.bfloat16)
    result = middle + jnp.dot(active, full_down, preferred_element_type=jnp.float32)
    output = result.astype(jnp.bfloat16).reshape(wins, local_len, width)
    grad_y = (d_out.astype(jnp.float32) * loss_weight[:, None, None]).reshape(rows, width)
    grad_ffn = grad_y.astype(jnp.bfloat16)
    raw_down = jnp.einsum("tf,td->fd", active, grad_ffn, preferred_element_type=jnp.float32)
    grad_act = jnp.einsum("td,fd->tf", grad_ffn, full_down, preferred_element_type=jnp.float32)
    gelu_pull = jax.vjp(jax.nn.gelu, up_proj)[1]
    grad_up = gelu_pull(grad_act)[0].astype(jnp.bfloat16)
    raw_up = jnp.einsum("td,tf->df", h_two, grad_up, preferred_element_type=jnp.float32)
    grad_h_two = jnp.einsum("tf,df->td", grad_up, full_up, preferred_element_type=jnp.float32)
    norm_pull = jax.vjp(layer_norm, middle, gains[2], gains[3])[1]
    grad_mid_ln, raw_gain_two, raw_shift_two = norm_pull(grad_h_two)
    grad_mid = grad_y + grad_mid_ln
    grad_att = grad_mid.astype(jnp.bfloat16)
    raw_out = jnp.einsum("td,te->de", attended, grad_att, preferred_element_type=jnp.float32)
    grad_o = jnp.einsum("te,de->td", grad_att, full_out, preferred_element_type=jnp.float32)
    grad_o = grad_o.astype(jnp.bfloat16).reshape(wins, blocks_dev, BLK, H, HD)
    grad_p = jnp.einsum("wbqhd,wkhd->wbhqk", grad_o, values, preferred_element_type=jnp.float32)
    prob_f = prob.astype(jnp.float32)
    inner = jnp.sum(prob_f * grad_p, axis=-1, keepdims=True)
    grad_s = (prob_f * (grad_p - inner)).astype(jnp.bfloat16)
    grad_q = (
        jnp.einsum("wbhqk,wkhd->wbqhd", grad_s, keys, preferred_element_type=jnp.float32)
        * inv_root
    )
    grad_v = jnp.einsum("wbhqk,wbqhd->wkhd", prob, grad_o, preferred_element_type=jnp.float32)
    grad_k = (
        jnp.einsum("wbhqk,wbqhd->wkhd", grad_s, q_heads, preferred_element_type=jnp.float32)
        * inv_root
    )
    grad_kv = jnp.stack([grad_k, grad_v], axis=2).astype(jnp.bfloat16)
    grad_kv = lax.psum_scatter(
        grad_kv.reshape(wins, block_count * BLK, 2 * width),
        "seq",
        scatter_dimension=1,
        tiled=True,
    ).reshape(rows, 2 * width)
    grad_qkv = jnp.concatenate(
        [grad_q.reshape(rows, width).astype(jnp.bfloat16), grad_kv], axis=1
    )
    raw_qkv = jnp.einsum("td,te->de", h_one, grad_qkv, preferred_element_type=jnp.float32)
    grad_h_one = jnp.einsum("te,de->td", grad_qkv, full_qkv, preferred_element_type=jnp.float32)
    first_pull = jax.vjp(layer_norm, tokens, gains[0], gains[1])[1]
    grad_tok_ln, raw_gain_one, raw_shift_one = first_pull(grad_h_one)
    d_input = (grad_mid + grad_tok_ln).reshape(wins, local_len, width)
    raw_norm = jnp.concatenate([raw_gain_one, raw_shift_one, raw_gain_two, raw_shift_two])
    red_qkv, red_out, red_up, red_down = (
        lax.psum_scatter(
            lax.psum_scatter(raw.astype(jnp.bfloat16), "seq", scatter_dimension=0, tiled=True),
            "win",
            scatter_dimension=1,
            tiled=True,
        ).astype(jnp.float32)
        for raw in (raw_qkv, raw_out, raw_up, raw_down)
    )
    red_norm = lax.psum_scatter(raw_norm, ("win", "seq"), scatter_dimension=0, tiled=True)
    reduced = (red_qkv, red_out, red_up, red_down, red_norm)
    local_squares = jnp.float32(0.0)
    for grad in reduced:
        local_squares = local_squares + jnp.sum(grad * grad)
    grad_norm = jnp.sqrt(lax.psum(local_squares, ("win", "seq")))
    factor = 1.0 / jnp.maximum(grad_norm, 1.0)
    clipped = tuple((grad * factor for grad in reduced))
    count = jnp.float32(STEP)
    fix_one = 1.0 - jnp.power(jnp.float32(beta_one), count)
    fix_two = 1.0 - jnp.power(jnp.float32(beta_two), count)
    params = (w_qkv, w_out, w_up, w_down, norm_params)
    firsts = (m_qkv, m_out, m_up, m_down, m_norm)
    seconds = (v_qkv, v_out, v_up, v_down, v_norm)
    rates = (rate_matrix, rate_output, rate_matrix, rate_matrix, rate_norm)
    news, moms, secs = ([], [], [])
    for index in range(5):
        decay = 0.0 if index == 4 else decay_rate
        new_w, new_m, new_v = adam_update(
            params[index],
            clipped[index],
            firsts[index],
            seconds[index],
            rates[index],
            decay,
            fix_one,
            fix_two,
        )
        news.append(new_w)
        moms.append(new_m)
        secs.append(new_v)
    return (
        output,
        d_input,
        clipped[0],
        clipped[1],
        clipped[2],
        clipped[3],
        clipped[4],
        news[0],
        news[1],
        news[2],
        news[3],
        news[4],
        moms[0],
        moms[1],
        moms[2],
        moms[3],
        moms[4],
        secs[0],
        secs[1],
        secs[2],
        secs[3],
        secs[4],
        grad_norm.reshape(1),
    )


def solution(mesh):
    placed = (
        P("win", "seq", None),
        P("win", "seq", None),
        P("win", "seq", None, None),
        P("win"),
        P("seq", "win"),
        P("seq", "win"),
        P("seq", "win"),
        P("seq", "win"),
        P(("win", "seq")),
        P("seq", "win"),
        P("seq", "win"),
        P("seq", "win"),
        P("seq", "win"),
        P(("win", "seq")),
        P("seq", "win"),
        P("seq", "win"),
        P("seq", "win"),
        P("seq", "win"),
        P(("win", "seq")),
    )
    return jax.shard_map(
        per_device,
        mesh=mesh,
        in_specs=placed,
        out_specs=(
            P("win", "seq", None),
            P("win", "seq", None),
            P("seq", "win"),
            P("seq", "win"),
            P("seq", "win"),
            P("seq", "win"),
            P(("win", "seq")),
            P("seq", "win"),
            P("seq", "win"),
            P("seq", "win"),
            P("seq", "win"),
            P(("win", "seq")),
            P("seq", "win"),
            P("seq", "win"),
            P("seq", "win"),
            P("seq", "win"),
            P(("win", "seq")),
            P("seq", "win"),
            P("seq", "win"),
            P("seq", "win"),
            P("seq", "win"),
            P(("win", "seq")),
            P(),
        ),
        check_vma=False,
    )
```

time: 1230 us -> 690 us (0.56)
  waiting for transfers between devices: 631 us -> 286 us
  local copies, waits for them, and re-layouts: 238 us -> 69 us
  other arithmetic: 145 us -> 41.1 us
  blocking collectives: 111 us -> 185 us
    reduce_scatter x5, waiting for transfers between devices: 277 us -> 139 us  [the longest x4 117 us: per_device(): lax.psum_scatter(raw.astype(jnp.bfloat16), 'seq', scatter_dimension=0, ti...]
    while x4 -> x0, waiting for transfers between devices: 92 us -> none
    all_gather x6 -> x4, waiting for transfers between devices: 137 us -> 45.8 us  [per_device(): lax.all_gather(lax.all_gather(low, 'win', axis=1, tiled=True), 'seq', axi...]
    scatter-add x2 -> x0, other arithmetic: 80.8 us -> none  [send_back(): buffer = jnp.zeros((block_count, BLK, 2, H, HD), jnp.float32).at[index, :...]
    gather x3 -> x0, local copies, waits for them, and re-layouts: 56.6 us -> none  [pick_slots(): return source[win_ix, index, :, :, head_ix]]
    while x14 -> x0, local copies, waits for them, and re-layouts: 44.2 us -> none
    unnamed x3 -> x2, blocking collectives: 36.3 us -> 79.3 us
    reshape x7 -> x6, local copies, waits for them, and re-layouts: 44.8 us -> 5.58 us  [the longest x2 3.14 us: per_device(): grad_o = grad_o.astype(jnp.bfloat16).reshape(wins, blocks_dev, BLK, H, HD)]
  transfers between devices with their start and end apart: 19 -> 14, of which waited for: 16 -> 10; matrix products, arithmetic and copies ran while one was open for 16% -> 23% of each run, Pallas kernels for 0% -> 0%
where the time goes in v1:
time: 690 us; the launch traced here: 681 us
  waiting for transfers between devices  286 us (41%)
  blocking collectives  185 us (27%)
  matrix products  78.7 us (11%)
  local copies, waits for them, and re-layouts  69 us (10%)
  other arithmetic  41.1 us (6%)
  between operations  19.9 us (3%)
    reduce_scatter x4, waiting for transfers between devices, per_device(): lax.psum_scatter(raw.astype(jnp.bfloat16), 'seq', scatter_dimension=0, ti...  117 us
    unnamed x2, blocking collectives  79.3 us
    unnamed x18, waiting for transfers between devices  78.1 us
    all_gather x4, blocking collectives, per_device(): lax.all_gather(low, 'win', axis=1, tiled=True)  64.6 us
    unnamed x89, local copies, waits for them, and re-layouts  52.3 us
    all_gather x4, waiting for transfers between devices, per_device(): lax.all_gather(lax.all_gather(low, 'win', axis=1, tiled=True), 'seq', axi...  45.8 us
    psum x1, blocking collectives, per_device(): grad_norm = jnp.sqrt(lax.psum(local_squares, ('win', 'seq')))  40.8 us
    all_gather x1, waiting for transfers between devices, per_device(): window = lax.all_gather(keyval, 'seq', axis=1, tiled=True)  23.8 us
  transfers between devices with their start and end apart: 14, of which 10 were waited for; matrix products, arithmetic and copies ran while one was open for 23% of the time, Pallas kernels for 0%

profile of v1, /device:TPU:0, one launch (start us, length us, event | category | flops | bytes accessed | tf_op | source)
XLA Modules:
  0.0 680.8 jit_solution(3838037226972411840)
XLA Ops:
  8.3 17.0 %all-gather = bf16[4,576,96]{1,2,0:T(8,128)(2,1)S(1)} all-gather(bf16[1,576,96]{1,2,0:T(8,128)(2,1)S(1)} %convert_bitcast_fusion), channel_id=1, replica_groups=mesh['win'=4,'seq'=8] {'win'}, dimensions={0}, use_global_device_ids=true | all-gather | bytes 552960 | tf_op jit(solution)/shard_map/all_gather | solution.py:81
  26.8 17.4 %all_gather.38 = bf16[384,768]{0,1:T(8,128)(2,1)} all-gather(bf16[384,192]{0,1:T(8,128)(2,1)S(1)} %convert_element_type.148), channel_id=1, replica_groups=mesh['win'=4,'seq'=8] {'win'}, dimensions={1}, use_global_device_ids=true | all-gather | bytes 737280 | tf_op jit(solution)/shard_map/all_gather | solution.py:81
  44.6 39.8 %all-reduce = bf16[3072]{0:T(1024)(128)(2,1)S(1)} all-reduce(bf16[3072]{0:T(1024)(128)(2,1)S(1)} %dynamic-update-slice), channel_id=1, replica_groups=mesh['win'=4,'seq'=8] {'win','seq'}, use_global_device_ids=true, to_apply=%add | all-reduce | flops 3072 | bytes 12288
  90.3 14.1 %all_gather.34 = bf16[96,768]{0,1:T(8,128)(2,1)S(1)} all-gather(bf16[96,192]{0,1:T(8,128)(2,1)S(1)} %copy.161), channel_id=1, replica_groups=mesh['win'=4,'seq'=8] {'win'}, dimensions={1}, use_global_device_ids=true | all-gather | bytes 184320 | tf_op jit(solution)/shard_map/all_gather | solution.py:81
  105.3 16.1 %all_gather.36 = bf16[96,3072]{1,0:T(8,128)(2,1)} all-gather(bf16[96,768]{1,0:T(8,128)(2,1)S(1)} %convert_element_type.146), channel_id=1, replica_groups=mesh['win'=4,'seq'=8] {'win'}, dimensions={1}, use_global_device_ids=true | all-gather | bytes 737280 | tf_op jit(solution)/shard_map/all_gather | solution.py:81
  125.2 5.4 fusion.66
  130.6 23.8 %all-gather.9.cloned.1.call-done = bf16[2,1024,1536]{1,2,0:T(8,128)(2,1)} async-done(((bf16[2,128,1536]{1,2,0:T(8,128)(2,1)}), bf16[2,1024,1536]{1,2,0:T(8,128)(2,1)}) %all-gather.9.cloned.1.call-update) | async-done | bytes 6291472 | tf_op jit(solution)/shard_map/all_gather | solution.py:95
  154.4 3.7 fusion.17
  165.0 7.3 %fusion.30 = bf16[2,2,64,12,64]{2,4,1,3,0:T(8,128)(2,1)S(1)} fusion(bf16[2,2,12,64,1024]{4,3,1,2,0:T(8,128)(2,1)S(1)} %exponential_convert_fusion, bf16[2,1024,2,12,64]{1,4,3,2,0:T(8,128)(2,1)} %bitcast.173), kind=kOutput, calls=%fused_computation.43 | convolution fusion | flops 402849792 | bytes 9830400 | tf_op jit(solution)/shard_map/wbhqk,wkhd->wbqhd/dot_general | solution.py:106
  173.6 7.1 %all-gather.11.cloned.1.call-done = bf16[768,768]{1,0:T(8,128)(2,1)} async-done(((bf16[96,768]{1,0:T(8,128)(2,1)}), bf16[768,768]{1,0:T(8,128)(2,1)}) %all-gather.11.cloned.1.call-update) | async-done | bytes 1179664 | tf_op jit(solution)/shard_map/all_gather | solution.py:81
  182.9 38.6 %all-gather.13.cloned.1.call-done = bf16[768,3072]{1,0:T(8,128)(2,1)} async-done(((bf16[96,3072]{1,0:T(8,128)(2,1)}), bf16[768,3072]{1,0:T(8,128)(2,1)}) %all-gather.13.cloned.1.call-update) | async-done | bytes 4718608 | tf_op jit(solution)/shard_map/all_gather | solution.py:81
  221.4 7.8 %fusion.10 = (bf16[256,3072]{1,0:T(8,128)(2,1)S(1)}, f32[256,3072]{1,0:T(8,128)}) fusion(f32[256,3072]{1,0:T(8,128)} %fusion.66, bf16[768,3072]{1,0:T(8,128)(2,1)} %all-gather.13.cloned.1.call-done, f32[256,768]{1,0:T(8,128)S(1)} %get-tuple-element.196, f32[768]{0:T(1024)S(1)} %get-tuple-element.190, f32[768]{0:T(1024)S(1)} %get-tuple-element.189, ...), kind=kOutput, calls=%fused_computation.24 | convolution fusion | flops 1224671232 | bytes 13377536 | tf_op jit(solution)/shard_map/dot_general | solution.py:110
  232.9 6.3 convolution_convert_fusion
  239.3 5.2 convolution_convert_fusion.1
  250.0 5.7 fusion.12
  255.7 6.3 fusion.13
  261.9 7.8 %fusion = f32[2,2,12,64]{3,1,2,0:T(2,128)S(1)} fusion(f32[2,2,12,64,1024]{4,3,1,2,0:T(8,128)} %bitcast.165, bf16[2,2,12,64,1024]{4,3,1,2,0:T(8,128)(2,1)} %copy-done.1), kind=kLoop, calls=%fused_computation.2 | loop fusion | flops 9434112 | bytes 18886656 | tf_op jit(solution)/shard_map/reduce_sum | solution.py:131
  269.7 9.6 %fusion.1 = bf16[2,2,12,64,1024]{4,3,1,2,0:T(8,128)(2,1)S(1)} fusion(f32[2,2,12,64]{3,1,2,0:T(2,128)S(1)} %fusion, f32[2,12,1024,128]{2,3,1,0} %fusion.13, f32[2,2,12,64]{3,1,2,0:T(2,128)S(1)} %bitcast.188, f32[2,2,12,1024]{3,1,2,0:T(2,128)S(1)} %copy-done.8, f32[2,12,1024,128]{2,3,1,0} %copy-done), kind=kLoop, calls=%fused_computation.3 | loop fusion | flops 25165824 | bytes 31678464 | tf_op jit(solution)/shard_map/convert_element_type | solution.py:132
  284.9 3.4 copy.168
  288.3 16.6 %copy.184 = bf16[2,1024,1536]{2,0,1:T(2,128)(2,1)} copy(bf16[2,1024,1536]{1,2,0:T(8,128)(2,1)} %bitcast.167) | data formatting | bytes 12582912
  304.9 7.2 %copy.200 = bf16[128,8,2,1536]{3,1,2,0:T(8,128)(2,1)} copy(bf16[128,8,2,1536]{3,2,1,0:T(2,128)(2,1)} %bitcast.168) | data formatting | bytes 12582912
  313.9 13.7 %reduce-scatter.26.cloned.1.call-done = bf16[384,768]{1,0:T(8,128)(2,1)} async-done(((bf16[3072,768]{1,0:T(8,128)(2,1)}), bf16[384,768]{1,0:T(8,128)(2,1)}) %reduce-scatter.26.cloned.1.call-update) | async-done | bytes 589840 | tf_op jit(solution)/shard_map/reduce_scatter | solution.py:160
  329.8 55.2 %reduce-scatter.22.cloned.1.call-done = bf16[96,3072]{1,0:T(8,128)(2,1)} async-done(((bf16[768,3072]{1,0:T(8,128)(2,1)}), bf16[96,3072]{1,0:T(8,128)(2,1)}) %reduce-scatter.22.cloned.1.call-update) | async-done | bytes 589840 | tf_op jit(solution)/shard_map/reduce_scatter | solution.py:160
  385.2 6.9 %fusion.33 = bf16[2,2,64,12,64]{2,4,1,3,0:T(8,128)(2,1)S(1)} fusion(bf16[2,2,12,64,1024]{4,3,1,2,0:T(8,128)(2,1)} %copy-done.2, bf16[2,1024,2,12,64]{1,4,3,2,0:T(8,128)(2,1)} %bitcast.174), kind=kOutput, calls=%fused_computation.44 | convolution fusion | flops 403046400 | bytes 9830400 | tf_op jit(solution)/shard_map/wbhqk,wkhd->wbqhd/dot_general | solution.py:134
  396.3 54.2 %reduce-scatter.28.cloned.1.call-done = bf16[128,3072]{1,0:T(8,128)(2,1)} async-done(((bf16[1024,3072]{1,0:T(8,128)(2,1)}), bf16[128,3072]{1,0:T(8,128)(2,1)}) %reduce-scatter.28.cloned.1.call-update) | async-done | bytes 786448
  455.0 3.9 convolution_convert_fusion.2
  463.8 6.1 fusion.36
  474.1 21.1 %reduce-scatter.34.cloned.1.call-done = bf16[192,384]{1,0:T(8,128)(2,1)} async-done(((bf16[768,384]{1,0:T(8,128)(2,1)}), bf16[192,384]{1,0:T(8,128)(2,1)}) %reduce-scatter.34.cloned.1.call-update) | async-done | bytes 147472
  496.2 21.6 %reduce-scatter.24.cloned.1.call-done = bf16[96,768]{1,0:T(8,128)(2,1)} async-done(((bf16[96,3072]{1,0:T(8,128)(2,1)}), bf16[96,768]{1,0:T(8,128)(2,1)}) %reduce-scatter.24.cloned.1.call-update) | async-done | bytes 147472 | tf_op jit(solution)/shard_map/reduce_scatter | solution.py:159
  520.0 48.1 %reduce-scatter.18.cloned.1.call-done = bf16[96,2304]{1,0:T(8,128)(2,1)} async-done(((bf16[768,2304]{1,0:T(8,128)(2,1)}), bf16[96,2304]{1,0:T(8,128)(2,1)}) %reduce-scatter.18.cloned.1.call-update) | async-done | bytes 442384 | tf_op jit(solution)/shard_map/reduce_scatter | solution.py:160
  574.1 39.5 %all-reduce.1 = f32[3072]{0:T(1024)S(1)} all-reduce(f32[3072]{0:T(1024)S(1)} %pad_maximum_fusion.4), channel_id=11, replica_groups=mesh['win'=4,'seq'=8] {'win','seq'}, use_global_device_ids=true, to_apply=%region_29.30.clone | all-reduce | flops 3072 | bytes 24576
  622.0 40.8 %psum.7 = f32[]{:T(128)} all-reduce(f32[]{:T(128)S(6)} %add.254), channel_id=1, replica_groups=mesh['win'=4,'seq'=8] {'win','seq'}, use_global_device_ids=true, to_apply=%region_31.32 | all-reduce | flops 1 | bytes 8 | tf_op jit(solution)/shard_map/psum | solution.py:172
  (189 shorter events, 83.9 us)
Async XLA Ops:
  7.2 19.6 %copy-start.16 = (f32[384,192]{0,1:T(8,128)S(1)}, f32[384,192]{0,1:T(8,128)}, u32[]{:S(2)}) copy-start(f32[384,192]{0,1:T(8,128)} %param.26) | copy-start | bytes 884740
  7.2 37.1 %copy-start.27 = (f32[96]{0:T(128)S(1)}, f32[96]{0:T(128)}, u32[]{:S(2)}) copy-start(f32[96]{0:T(128)} %param.27) | copy-start | bytes 1156
  7.2 77.1 %copy-start.3 = (bf16[2,128,768]{2,1,0:T(8,128)(2,1)S(1)}, bf16[2,128,768]{2,1,0:T(8,128)(2,1)}, u32[]{:S(2)}) copy-start(bf16[2,128,768]{2,1,0:T(8,128)(2,1)} %param.19) | copy-start | bytes 1179652
  7.2 77.8 %all-gather.7.cloned.1.call-start = ((), (), s32[]{:S(2)}) async-start(), calls=%async_computation.9 | async-start | bytes 3981312 | tf_op jit(solution)/shard_map/all_gather | solution.py:81
  26.7 98.3 %all-gather.15.cloned.1.call-start = ((), (), s32[]{:S(2)}) async-start(), calls=%async_computation.13 | async-start | bytes 5308416 | tf_op jit(solution)/shard_map/all_gather | solution.py:81
  44.2 110.2 %all-gather.9.cloned.1.call-start = ((), (), s32[]{:S(2)}) async-start(), calls=%async_computation.10 | async-start | bytes 7077888 | tf_op jit(solution)/shard_map/all_gather | solution.py:95
  88.8 16.4 %copy-start.14 = (f32[96,768]{1,0:T(8,128)S(1)}, f32[96,768]{1,0:T(8,128)}, u32[]{:S(2)}) copy-start(f32[96,768]{1,0:T(8,128)} %param.25) | copy-start | bytes 884740
  88.9 32.6 %copy-start.31 = (s32[2]{0:T(128)S(1)}, s32[2]{0:T(128)}, u32[]{:S(2)}) copy-start(s32[2]{0:T(128)} %param.22) | copy-start | bytes 28
  88.9 32.7 %copy-start.26 = (s32[2,2,12,3]{2,1,3,0:T(2,128)S(1)}, s32[2,2,12,3]{2,1,3,0:T(2,128)}, u32[]{:S(2)}) copy-start(s32[2,2,12,3]{2,1,3,0:T(2,128)} %param.21) | copy-start | bytes 1732
  88.9 33.4 %copy-start.22 = (bf16[2,128,768]{2,1,0:T(8,128)(2,1)S(1)}, bf16[2,128,768]{2,1,0:T(8,128)(2,1)}, u32[]{:S(2)}) copy-start(bf16[2,128,768]{2,1,0:T(8,128)(2,1)} %param.20) | copy-start | bytes 1179652
  90.1 90.6 %all-gather.11.cloned.1.call-start = ((), (), s32[]{:S(2)}) async-start(), calls=%async_computation.11 | async-start | bytes 1327104 | tf_op jit(solution)/shard_map/all_gather | solution.py:81
  105.2 116.3 %all-gather.13.cloned.1.call-start = ((), (), s32[]{:S(2)}) async-start(), calls=%async_computation.12 | async-start | bytes 5308416 | tf_op jit(solution)/shard_map/all_gather | solution.py:81
  121.5 190.7 %reduce-scatter.20.cloned.1.call-start = ((), (), s32[]{:S(2)}) async-start(), calls=%async_computation.15 | async-start | bytes 1327104 | tf_op jit(solution)/shard_map/reduce_scatter | solution.py:160
  122.3 40.2 %copy-start.7 = (f32[2,2,12,1024]{3,1,2,0:T(2,128)}, f32[2,2,12,1024]{3,1,2,0:T(2,128)S(1)}, u32[]{:S(2)}) copy-start(f32[2,2,12,1024]{3,1,2,0:T(2,128)S(1)} %add.238) | copy-start | bytes 589828
  232.9 94.7 %reduce-scatter.26.cloned.1.call-start = ((), (), s32[]{:S(2)}) async-start(), calls=%async_computation.18 | async-start | bytes 5308416 | tf_op jit(solution)/shard_map/reduce_scatter | solution.py:160
  239.2 145.7 %reduce-scatter.22.cloned.1.call-start = ((), (), s32[]{:S(2)}) async-start(), calls=%async_computation.16 | async-start | bytes 5308416 | tf_op jit(solution)/shard_map/reduce_scatter | solution.py:160
  244.5 206.0 %reduce-scatter.28.cloned.1.call-start = ((), (), s32[]{:S(2)}) async-start(), calls=%async_computation.19 | async-start | bytes 7077888
  312.1 160.5 %reduce-scatter.32.cloned.1.call-start = ((), (), s32[]{:S(2)}) async-start(), calls=%async_computation.21 | async-start | bytes 245760
  313.9 181.2 %reduce-scatter.34.cloned.1.call-start = ((), (), s32[]{:S(2)}) async-start(), calls=%async_computation.22 | async-start | bytes 737280
  329.8 188.0 %reduce-scatter.24.cloned.1.call-start = ((), (), s32[]{:S(2)}) async-start(), calls=%async_computation.17 | async-start | bytes 737280 | tf_op jit(solution)/shard_map/reduce_scatter | solution.py:159
  385.0 183.2 %reduce-scatter.18.cloned.1.call-start = ((), (), s32[]{:S(2)}) async-start(), calls=%async_computation.14 | async-start | bytes 3981312 | tf_op jit(solution)/shard_map/reduce_scatter | solution.py:160
  392.1 62.9 %copy-start.10 = (bf16[256,768]{1,0:T(8,128)(2,1)S(1)}, bf16[256,768]{1,0:T(8,128)(2,1)}, u32[]{:S(2)}) copy-start(bf16[256,768]{1,0:T(8,128)(2,1)} %copy-done.9) | copy-start | bytes 1179652
  458.9 155.4 %reduce-scatter.30.cloned.1.call-start = ((), (), s32[]{:S(2)}) async-start(), calls=%async_computation.20 | async-start | bytes 737280
  573.6 90.0 %copy-start.11 = (f32[384,192]{1,0:T(8,128)S(1)}, f32[384,192]{1,0:T(8,128)}, u32[]{:S(2)}) copy-start(f32[384,192]{1,0:T(8,128)} %copy.171) | copy-start | bytes 884740
  573.6 90.0 %copy-start.12 = (f32[384,192]{1,0:T(8,128)S(1)}, f32[384,192]{1,0:T(8,128)}, u32[]{:S(2)}) copy-start(f32[384,192]{1,0:T(8,128)} %copy.172) | copy-start | bytes 884740
  622.0 45.5 %copy-start.28 = (f32[96]{0:T(128)S(1)}, f32[96]{0:T(128)}, u32[]{:S(2)}) copy-start(f32[96]{0:T(128)} %param.37) | copy-start | bytes 1156
  622.0 45.5 %copy-start.29 = (f32[96]{0:T(128)S(1)}, f32[96]{0:T(128)}, u32[]{:S(2)}) copy-start(f32[96]{0:T(128)} %param.32) | copy-start | bytes 1156
  622.0 46.1 %copy-start.21 = (f32[96,192]{1,0:T(8,128)S(1)}, f32[96,192]{1,0:T(8,128)}, u32[]{:S(2)}) copy-start(f32[96,192]{1,0:T(8,128)} %param.24) | copy-start | bytes 221188
  663.9 7.9 %copy-start.15 = (f32[96,768]{1,0:T(8,128)S(1)}, f32[96,768]{1,0:T(8,128)}, u32[]{:S(2)}) copy-start(f32[96,768]{1,0:T(8,128)} %param.25) | copy-start | bytes 884740
  663.9 7.9 %copy-start.19 = (bf16[96,768]{1,0:T(8,128)(2,1)S(1)}, bf16[96,768]{1,0:T(8,128)(2,1)}, u32[]{:S(2)}) copy-start(bf16[96,768]{1,0:T(8,128)(2,1)} %reduce-scatter.24.cloned.1.call-done) | copy-start | bytes 442372
  664.0 7.9 %copy-start.24 = (f32[96,768]{1,0:T(8,128)S(1)}, f32[96,768]{1,0:T(8,128)}, u32[]{:S(2)}) copy-start(f32[96,768]{1,0:T(8,128)} %param.35) | copy-start | bytes 884740
  664.0 7.9 %copy-start.25 = (f32[96,768]{1,0:T(8,128)S(1)}, f32[96,768]{1,0:T(8,128)}, u32[]{:S(2)}) copy-start(f32[96,768]{1,0:T(8,128)} %param.30) | copy-start | bytes 884740
  (16 other events, 65.4 us)
Sparse Core Ops, SparseCore 0:
  26.8 36.0 all-gather.6
  64.8 40.3 all-gather.14
  107.7 46.6 all-gather.8
  156.7 24.0 all-gather.10
  182.5 38.9 all-gather.12
  233.0 36.7 reduce-scatter.19
  273.7 53.8 reduce-scatter.25
  331.1 53.8 reduce-scatter.21
  388.7 61.7 reduce-scatter.27
  453.2 19.3 reduce-scatter.31
  474.9 20.1 reduce-scatter.33
  497.4 20.3 reduce-scatter.23
  521.6 46.4 reduce-scatter.17
  571.0 21.9 reduce-scatter.29

commit v2 on v1

--- a/solution.py
+++ b/solution.py
@@ -1,8 +1,12 @@
+import functools
 import math
+from typing import Any, NamedTuple
 
 import jax
 import jax.numpy as jnp
 from jax import lax
+from jax.experimental import pallas as pl
+from jax.experimental.pallas import tpu as pltpu
 from jax.sharding import PartitionSpec as P
 
 H = 12
@@ -20,6 +24,7 @@
 rate_matrix = 0.04
 rate_output = 0.16
 rate_norm = 0.6
+VMEM_LIMIT = 63 << 20
 
 
 def layer_norm(values, gain, shift):
@@ -222,6 +227,879 @@
     )
 
 
+MESH = pl.DeviceIdType.MESH
+F32, BF16 = jnp.float32, jnp.bfloat16
+GELU_C = math.sqrt(2.0 / math.pi)
+NT = (((1,), (1,)), ((), ()))
+TN = (((0,), (0,)), ((), ()))
+
+
+def dot(a, b):
+    return jnp.dot(a, b, preferred_element_type=F32)
+
+
+def dot_nt(a, b):
+    return lax.dot_general(a, b, NT, preferred_element_type=F32)
+
+
+def dot_tn(a, b):
+    return lax.dot_general(a, b, TN, preferred_element_type=F32)
+
+
+def remote(src, dst, sems, k, dev):
+    return pltpu.make_async_remote_copy(
+        src_ref=src, dst_ref=dst, send_sem=sems[0].at[k], recv_sem=sems[1].at[k], device_id=dev, device_id_type=MESH
+    )
+
+
+class Place:
+    def __init__(self):
+        self.w = lax.axis_index("win")
+        self.s = s = lax.axis_index("seq")
+        self.c = c = s % 2
+        x = (s // 2) % 2
+        y = s // 4
+        dx, dy = 2 - 4 * x, 4 - 8 * y
+        self.turn = 1 - 2 * c
+        self.n1 = s + (1 - c) * dx + c * dy
+        self.n2 = s + (1 - c) * dy + c * dx
+        self.nd = s + dx + dy
+        self.par = s + self.turn
+        self.roles = (s, self.n1, self.n2, self.nd)
+        self.par_roles = tuple(r + self.turn for r in (s, self.n2, self.n1, self.nd))
+
+
+class Blocks:
+    def __init__(self, buf, seq_first=False, start=0, count=None):
+        self.buf, self.seq_first, self.rows = buf, seq_first, pl.ds(start, buf.shape[3] if count is None else count)
+
+    def block(self, w, s):
+        return self.buf.at[(s // 2, s % 2, w, self.rows) if self.seq_first else (w, s // 2, s % 2, self.rows)]
+
+    def read(self, w, s):
+        return self.buf[(s // 2, s % 2, w, self.rows) if self.seq_first else (w, s // 2, s % 2, self.rows)]
+
+    def group(self, s):
+        every = slice(None)
+        return self.buf.at[(s // 2, s % 2, every, self.rows) if self.seq_first else (every, s // 2, s % 2, self.rows)]
+
+    def core(self, c, w=slice(None)):
+        return self.buf.at[:, c, w, self.rows]
+
+
+class Gather:
+    def __init__(self, place, blocks, sems):
+        self.p, self.b, self.sems = place, blocks, sems
+
+    def push(self, s, k, to):
+        remote(self.b.group(s), self.b.group(s), self.sems, k, (self.p.w, to)).start()
+
+    def got(self, s, k):
+        remote(self.b.group(s), self.b.group(s), self.sems, k, (self.p.w, self.p.par)).wait_recv()
+
+    def along(self, dz, w):
+        block = self.b.block(w, self.p.s)
+        return remote(block, block, self.sems, dz - 1, ((self.p.w + dz) % 4, self.p.s))
+
+    def z_send(self):
+        for dz in (1, 2, 3):
+            self.along(dz, self.p.w).start()
+
+    def stage1(self):
+        p = self.p
+        for dz in (1, 2, 3):
+            self.along(dz, (p.w + 4 - dz) % 4).wait_recv()
+        self.push(p.s, 3, p.n1)
+        self.push(p.s, 4, p.n2)
+        self.push(p.s, 6, p.par)
+
+    def stage2(self):
+        p = self.p
+        self.got(p.n1, 3)
+        self.push(p.n1, 5, p.n2)
+        self.push(p.n1, 7, p.par)
+
+    def stage3(self):
+        p = self.p
+        self.got(p.n2, 4)
+        self.push(p.n2, 8, p.par)
+        self.got(p.nd, 5)
+        self.push(p.nd, 9, p.par)
+
+    def finish(self):
+        for k in range(4):
+            self.got(self.p.par_roles[k], 6 + k)
+
+    def drain(self):
+        p = self.p
+        for dz in (1, 2, 3):
+            self.along(dz, p.w).wait_send()
+        for k, s in ((3, p.s), (4, p.s), (6, p.s), (5, p.n1), (7, p.n1), (8, p.n2), (9, p.nd)):
+            remote(self.b.group(s), self.b.group(s), self.sems, k, (p.w, p.par)).wait_send()
+
+
+class PlaneGather:
+    def __init__(self, place, blocks, sems):
+        self.p, self.b, self.sems = place, blocks, sems
+
+    def one(self, s, k, to):
+        return remote(self.b.block(self.p.w, s), self.b.block(self.p.w, s), self.sems, k, (self.p.w, to))
+
+    def layer(self, c, w, k, dev):
+        return remote(self.b.core(c, w), self.b.core(c, w), self.sems, k, dev)
+
+    def stage1(self):
+        p = self.p
+        self.one(p.s, 3, p.n1).start()
+        self.one(p.s, 4, p.n2).start()
+
+    def stage2(self):
+        p = self.p
+        self.one(p.n1, 3, p.n1).wait_recv()
+        self.one(p.n1, 5, p.n2).start()
+
+    def stage3(self):
+        p = self.p
+        self.one(p.n2, 4, p.n2).wait_recv()
+        self.one(p.nd, 5, p.n2).wait_recv()
+        for dz in (1, 2, 3):
+            self.layer(p.c, p.w, dz - 1, ((p.w + dz) % 4, p.s)).start()
+        self.layer(p.c, p.w, 6, (p.w, p.par)).start()
+
+    def stage4(self):
+        p = self.p
+        for dz in (1, 2, 3):
+            w = (p.w + 4 - dz) % 4
+            self.layer(p.c, w, dz - 1, (w, p.s)).wait_recv()
+            self.layer(p.c, w, 6 + dz, (p.w, p.par)).start()
+
+    def finish(self):
+        p = self.p
+        for dz in range(4):
+            self.layer(1 - p.c, (p.w + 4 - dz) % 4, 6 + dz, (p.w, p.par)).wait_recv()
+
+    def drain(self):
+        p = self.p
+        self.one(p.s, 3, p.n1).wait_send()
+        self.one(p.s, 4, p.n2).wait_send()
+        self.one(p.n1, 5, p.n2).wait_send()
+        for dz in (1, 2, 3):
+            self.layer(p.c, p.w, dz - 1, ((p.w + dz) % 4, p.s)).wait_send()
+        for dz in range(4):
+            self.layer(p.c, (p.w + 4 - dz) % 4, 6 + dz, (p.w, p.par)).wait_send()
+
+
+class Scatter:
+    def __init__(self, place, blocks, space, sems):
+        self.p, self.b, self.sems = place, blocks, sems
+        self.c, self.d, self.e, self.f = space
+
+    def copies_c(self):
+        p = self.p
+        return [remote(self.b.group(p.par_roles[k]), self.c.at[k], self.sems, k, (p.w, p.par)) for k in range(4)]
+
+    def copies_d(self):
+        p = self.p
+        return [remote(self.c.at[2 + k], self.d.at[k], self.sems, 4 + k, (p.w, p.n2)) for k in range(2)]
+
+    def copy_e(self):
+        p = self.p
+        return remote(self.c.at[1], self.e, self.sems, 6, (p.w, p.n1))
+
+    def copies_f(self):
+        p = self.p
+        return [
+            remote(self.c.at[0, (p.w + dz) % 4], self.f.at[dz - 1], self.sems, 6 + dz, ((p.w + dz) % 4, p.s))
+            for dz in (1, 2, 3)
+        ]
+
+    def stage_c(self):
+        for copy in self.copies_c():
+            copy.start()
+
+    def stage_d(self):
+        waits, sends = self.copies_c(), self.copies_d()
+        for k in (2, 3, 0, 1):
+            waits[k].wait_recv()
+            for w in range(4):
+                self.c[k, w] = self.c[k, w] + self.b.read(w, self.p.roles[k])
+            if k >= 2:
+                sends[k - 2].start()
+
+    def stage_e(self):
+        waits = self.copies_d()
+        for k in (1, 0):
+            waits[k].wait_recv()
+            for w in range(4):
+                self.c[k, w] = self.c[k, w] + self.d[k, w]
+            if k == 1:
+                self.copy_e().start()
+
+    def stage_f(self):
+        self.copy_e().wait_recv()
+        for w in range(4):
+            self.c[0, w] = self.c[0, w] + self.e[w]
+        for copy in self.copies_f():
+            copy.start()
+
+    def finish(self):
+        total = self.c[0, self.p.w].astype(F32)
+        for k, copy in enumerate(self.copies_f()):
+            copy.wait_recv()
+            total = total + self.f[k].astype(F32)
+        return total
+
+    def drain(self):
+        for copy in (*self.copies_c(), *self.copies_d(), self.copy_e(), *self.copies_f()):
+            copy.wait_send()
+
+
+class PlaneScatter:
+    def __init__(self, place, blocks, space, sems):
+        self.p, self.b, self.sems = place, blocks, sems
+        self.c, self.z, self.d, self.e = space
+
+    def copy_c(self):
+        p = self.p
+        return remote(self.b.core(1 - p.c), self.c, self.sems, 0, (p.w, p.par))
+
+    def copies_z(self):
+        p = self.p
+        return [
+            remote(self.c.at[:, (p.w + dz) % 4], self.z.at[dz - 1], self.sems, dz, ((p.w + dz) % 4, p.s)) for dz in (1, 2, 3)
+        ]
+
+    def copies_d(self):
+        p = self.p
+        return [remote(self.c.at[r // 2, p.w], self.d.at[k], self.sems, 4 + k, (p.w, p.n2)) for k, r in enumerate((p.n2, p.nd))]
+
+    def copy_e(self):
+        p = self.p
+        return remote(self.c.at[p.n1 // 2, p.w], self.e, self.sems, 6, (p.w, p.n1))
+
+    def stage_c(self):
+        self.copy_c().start()
+
+    def stage_z(self):
+        p = self.p
+        self.copy_c().wait_recv()
+        for w in range(4):
+            for chip in range(4):
+                self.c[chip, w] = self.c[chip, w] + self.b.read(w, 2 * chip + p.c)
+        for copy in self.copies_z():
+            copy.start()
+
+    def stage_d(self):
+        p = self.p
+        for k, copy in enumerate(self.copies_z()):
+            copy.wait_recv()
+            for chip in range(4):
+                self.c[chip, p.w] = self.c[chip, p.w] + self.z[k, chip]
+        for copy in self.copies_d():
+            copy.start()
+
+    def stage_e(self):
+        p = self.p
+        waits = self.copies_d()
+        for k, r in ((1, p.n1), (0, p.s)):
+            waits[k].wait_recv()
+            self.c[r // 2, p.w] = self.c[r // 2, p.w] + self.d[k]
+            if k == 1:
+                self.copy_e().start()
+
+    def finish(self):
+        p = self.p
+        self.copy_e().wait_recv()
+        return self.c[p.s // 2, p.w].astype(F32) + self.e[...].astype(F32)
+
+    def drain(self):
+        for copy in (self.copy_c(), *self.copies_z(), *self.copies_d(), self.copy_e()):
+            copy.wait_send()
+
+
+class Exchange:
+    def __init__(self, place, src, dst, sems):
+        self.p, self.src, self.dst, self.sems = place, src, dst, sems
+
+    def copy(self, ds):
+        p = self.p
+        to = (p.s + ds) % 8
+        return remote(self.src.at[to], self.dst.at[p.s], self.sems, ds, (p.w, to))
+
+    def own(self):
+        return pltpu.make_async_copy(self.src.at[self.p.s], self.dst.at[self.p.s], self.sems[1].at[0])
+
+    def start(self):
+        for ds in (6, 5, 3, 7, 4, 2, 1):
+            self.copy(ds).start()
+        self.own().start()
+
+    def wait(self):
+        p = self.p
+        self.own().wait()
+        for ds in range(1, 8):
+            back = (p.s + 8 - ds) % 8
+            remote(self.src.at[back], self.dst.at[back], self.sems, ds, (p.w, back)).wait_recv()
+
+    def drain(self):
+        for ds in range(1, 8):
+            self.copy(ds).wait_send()
+
+
+def norm_stats(values):
+    centre = values - jnp.mean(values, axis=-1, keepdims=True)
+    rstd = lax.rsqrt(jnp.mean(centre * centre, axis=-1, keepdims=True) + ln_eps)
+    return centre * rstd, rstd
+
+
+def norm_back(grad, hat, rstd, gain):
+    scaled = grad * gain
+    return rstd * (
+        scaled - jnp.mean(scaled, axis=-1, keepdims=True) - hat * jnp.mean(scaled * hat, axis=-1, keepdims=True)
+    )
+
+
+def rows_of(ref, index, rows):
+    value = ref[index]
+    return value.reshape(rows, value.shape[-1])
+
+
+def turned(value):
+    return jnp.transpose(value.astype(F32)).astype(BF16)
+
+
+class Space(NamedTuple):
+    gn: Any
+    gq: Any
+    go: Any
+    gu: Any
+    gd: Any
+    rn: Any
+    sn: Any
+    sq: Any
+    sr: Any
+    so: Any
+    su: Any
+    sd: Any
+    sp: Any
+    gather_sems: Any
+    scatter_sems: Any
+    exchange_sems: Any
+    sum_sems: Any
+    count_out: Any
+    counts: Any
+    bias: Any
+    sb: Any
+    rb: Any
+    qh: Any
+    kh: Any
+    vh: Any
+    prob: Any
+    ab: Any
+    at: Any
+    gor: Any
+    gb: Any
+    att: Any
+    wout: Any
+    turned: Any
+    turned_b: Any
+    gains: Any
+    hat_a: Any
+    hat_b: Any
+    rstd_a: Any
+    rstd_b: Any
+    h: Any
+    wide: Any
+    y: Any
+    gy: Any
+    back: Any
+    mid_grad: Any
+    gk: Any
+    gv: Any
+    square: Any
+    squares: Any
+
+
+def scratch():
+    def scatter(*block, kind=BF16):
+        return tuple(pltpu.VMEM((*lead, *block), kind) for lead in ((4, 4), (2, 4), (4,), (3,)))
+
+    def sems(count):
+        return (pltpu.SemaphoreType.DMA((count,)),) * 2
+
+    half = (96, 384)
+    rows, wide = (256, 768), (8, 64, 1152)
+    return Space(
+        gn=pltpu.VMEM((4, 4, 2, 8, 128), F32),
+        gq=pltpu.VMEM((4, 4, 2, 96, 576), BF16),
+        go=pltpu.VMEM((4, 4, 2, 48, 384), BF16),
+        gu=pltpu.VMEM((4, 4, 2, 96, 768), BF16),
+        gd=pltpu.VMEM((4, 2, 4, 192, 384), BF16),
+        rn=pltpu.VMEM((4, 4, 2, 8, 128), F32),
+        sn=scatter(8, 128, kind=F32),
+        sq=scatter(48, 576),
+        sr=scatter(48, 576),
+        so=scatter(48, 384),
+        su=scatter(96, 768),
+        sd=scatter(*half),
+        sp=tuple(pltpu.VMEM((*lead, *half), BF16) for lead in ((4, 4), (3, 4), (2,), ())),
+        gather_sems=tuple(sems(10) for _ in range(7)),
+        scatter_sems=tuple(sems(10) for _ in range(7)),
+        exchange_sems=tuple(sems(8) for _ in range(5)),
+        sum_sems=sems(32),
+        count_out=pltpu.VMEM((8, 8, 128), F32),
+        counts=pltpu.VMEM((8, 8, 128), F32),
+        bias=pltpu.VMEM((3, 4, 4, 1024), F32),
+        sb=pltpu.VMEM(wide, BF16),
+        rb=pltpu.VMEM(wide, BF16),
+        qh=pltpu.VMEM((3, 1024, 64), BF16),
+        kh=pltpu.VMEM((3, 1024, 64), BF16),
+        vh=pltpu.VMEM((3, 1024, 64), BF16),
+        prob=pltpu.VMEM((3, 1024, 1024), BF16),
+        ab=pltpu.VMEM((8, 64, 384), BF16),
+        at=pltpu.VMEM((8, 64, 384), BF16),
+        gor=pltpu.VMEM((8, 64, 384), BF16),
+        gb=pltpu.VMEM(wide, BF16),
+        att=pltpu.VMEM(rows, BF16),
+        wout=pltpu.VMEM((4, 2, 2, 48, 768), BF16),
+        turned=pltpu.VMEM((768, 256), BF16),
+        turned_b=pltpu.VMEM((768, 256), BF16),
+        gains=pltpu.VMEM((32, 768), F32),
+        hat_a=pltpu.VMEM(rows, F32),
+        hat_b=pltpu.VMEM(rows, F32),
+        rstd_a=pltpu.VMEM((256, 1), F32),
+        rstd_b=pltpu.VMEM((256, 1), F32),
+        h=pltpu.VMEM(rows, BF16),
+        wide=pltpu.VMEM((256, 2304), BF16),
+        y=pltpu.VMEM(rows, F32),
+        gy=pltpu.VMEM(rows, BF16),
+        back=pltpu.VMEM(rows, F32),
+        mid_grad=pltpu.VMEM(rows, F32),
+        gk=pltpu.VMEM((64, 1024), F32),
+        gv=pltpu.VMEM((64, 1024), F32),
+        square=pltpu.VMEM((8, 128), F32),
+        squares=pltpu.VMEM((32, 8, 128), F32),
+    )
+
+
+def kernel(tree, live, rand_ids, x, d_out, w_qkv, w_out, w_up, w_down, norm, output, d_input, red_q, red_o, red_u, red_d, red_n, total, *rest):
+    r = jax.tree.unflatten(tree, rest)
+    p = Place()
+    barrier = pltpu.get_barrier_semaphore()
+
+    def greet(k, _):
+        to = ((p.w + k // 8) % 4, (p.s + k % 8) % 8)
+        pl.semaphore_signal(barrier, inc=1, device_id=to, device_id_type=MESH)
+        return 0
+
+    lax.fori_loop(1, 32, greet, 0)
+
+    all_n, all_q, all_r = Blocks(r.gn), Blocks(r.gq, count=48), Blocks(r.gq, start=48, count=48)
+    all_o, all_u = Blocks(r.go), Blocks(r.gu)
+    all_d, all_p = Blocks(r.gd, True, count=96), Blocks(r.gd, True, start=96, count=96)
+    gathers = [Gather(p, b, m) for b, m in zip((all_n, all_q, all_r, all_o, all_u, all_d), r.gather_sems)]
+    gather_n, gather_q, gather_r, gather_o, gather_u, gather_d = gathers
+    gather_p = PlaneGather(p, all_p, r.gather_sems[6])
+    scatters = [
+        Scatter(p, b, space, m)
+        for b, space, m in zip(
+            (Blocks(r.rn), all_q, all_r, all_o, all_u, all_d), (r.sn, r.sq, r.sr, r.so, r.su, r.sd), r.scatter_sems
+        )
+    ]
+    scatter_n, scatter_q, scatter_r, scatter_o, scatter_u, scatter_d = scatters
+    scatter_p = PlaneScatter(p, all_p, r.sp, r.scatter_sems[6])
+    count_x = Exchange(p, r.count_out, r.counts, r.exchange_sems[0])
+    qkv_x = Exchange(p, r.sb, r.rb, r.exchange_sems[1])
+    att_x = Exchange(p, r.ab, r.at, r.exchange_sems[2])
+    gro_x = Exchange(p, r.ab, r.gor, r.exchange_sems[3])
+    gqkv_x = Exchange(p, r.sb, r.gb, r.exchange_sems[4])
+    chip, core = p.s // 2, p.c
+
+    r.gn[p.w, chip, core] = jnp.zeros((8, 128), F32)
+    r.gn[p.w, chip, core, 0:1, 0:96] = norm[...].astype(BF16).astype(F32)
+    r.gq[p.w, chip, core] = w_qkv[...].astype(BF16)
+    r.gd[chip, core, p.w] = w_down[...].astype(BF16)
+    pl.semaphore_wait(barrier, 31)
+    gather_n.z_send()
+    gather_q.z_send()
+    gather_r.z_send()
+    gather_p.stage1()
+    for k in range(2):
+        r.go[p.w, chip, core, :, 192 * k : 192 * k + 192] = w_out[48 * k : 48 * k + 48].astype(BF16)
+    gather_o.z_send()
+
+    lane = lax.broadcasted_iota(jnp.int32, (8, 128), 1)
+    sub = lax.broadcasted_iota(jnp.int32, (8, 128), 0)
+    here = 2 * p.s + sub % 2
+    fixed = (jnp.abs(lane - here) <= 1).astype(F32) + (lane == 0).astype(F32) + (lane == 15).astype(F32)
+    for v in range(2):
+        for group in range(4):
+            counts = fixed
+            for row in range(6):
+                head = 3 * group + row // 2
+                for k in range(3):
+                    drawn = rand_ids[v * 12 + head, 2 * k + row % 2]
+                    counts = counts + ((sub == row) & (lane == drawn)).astype(F32)
+            r.count_out[4 * v + group] = counts
+    count_x.start()
+    r.gu[p.w, chip, core] = w_up[...].astype(BF16)
+    gather_u.z_send()
+    gather_d.z_send()
+
+    hat, rstd = norm_stats(x[...].astype(F32))
+    r.hat_a[...] = hat
+    r.rstd_a[...] = rstd
+    gather_n.stage1()
+    gather_p.stage2()
+    gather_q.stage1()
+
+    count_x.wait()
+    spread = (
+        lax.broadcasted_iota(jnp.int32, (128, 1024), 1) // 64 == lax.broadcasted_iota(jnp.int32, (128, 1024), 0)
+    ).astype(BF16)
+    wide = dot(r.counts[...].reshape(64, 128).astype(BF16), spread)
+    wide = jnp.where(wide > 0.5, jnp.log(jnp.maximum(wide, 1.0)), NEG)
+    for src in range(8):
+        for head in range(3):
+            row = src * 8 + head * 2
+            at = 2 * (src % 2)
+            r.bias[head, src // 2, at : at + 2] = wide[row : row + 2]
+
+    gather_n.stage2()
+    gather_r.stage1()
+    gather_q.stage2()
+    gather_n.stage3()
+    gather_n.finish()
+    lane = lax.broadcasted_iota(jnp.int32, (128, 768), 1)
+    sub = lax.broadcasted_iota(jnp.int32, (128, 768), 0)
+    gains = jnp.zeros((32, 768), F32)
+    for s in range(8):
+        place = ((lane == sub + 96 * s) & (sub < 96)).astype(BF16)
+        gains = gains + dot(r.gn[:, s // 2, s % 2].reshape(32, 128).astype(BF16), place)
+    r.gains[...] = gains
+    r.h[...] = (r.hat_a[...] * r.gains[0:1] + r.gains[8:9]).astype(BF16)
+    gather_r.stage2()
+    gather_o.stage1()
+    gather_q.stage3()
+    gather_r.stage3()
+    gather_q.finish()
+    gather_r.finish()
+
+    for w in range(4):
+        part = dot(r.h[...], rows_of(r.gq, w, 768)).astype(BF16)
+        for k in range(3):
+            kind, group = divmod(3 * w + k, 4)
+            for v in range(2):
+                for j in range(2):
+                    row, at = 128 * v + 64 * j, 576 * j + 192 * kind
+                    r.sb[4 * v + group, :, at : at + 192] = part[row : row + 64, 192 * k : 192 * k + 192]
+    qkv_x.start()
+    gather_u.stage1()
+    gather_p.stage3()
+    gather_o.stage2()
+    gather_o.stage3()
+    gather_d.stage1()
+    qkv_x.wait()
+    for src in range(8):
+        for head in range(3):
+            for kind, ref in enumerate((r.qh, r.kh, r.vh)):
+                for j in range(2):
+                    row, at = 128 * src + 64 * j, 576 * j + 192 * kind + 64 * head
+                    ref[head, row : row + 64] = r.rb[src, :, at : at + 64]
+
+    for head in range(3):
+
+        def attend(c, _, head=head):
+            q0 = pl.multiple_of(c * 256, 256)
+            raw = dot_nt(r.qh[head, pl.ds(q0, 256)], r.kh[head]) * (1.0 / math.sqrt(HD))
+            score = (raw.reshape(4, 64, 1024) + r.bias[head, c][:, None, :]).reshape(256, 1024)
+            prob = jnp.exp(score - jnp.max(score, axis=-1, keepdims=True))
+            prob = (prob * (1.0 / jnp.sum(prob, axis=-1, keepdims=True))).astype(BF16)
+            r.prob[head, pl.ds(q0, 256)] = prob
+            got = dot(prob, r.vh[head]).astype(BF16).reshape(2, 2, 64, 64)
+            for j in range(2):
+                at = 192 * j + 64 * head
+                r.ab[pl.ds(2 * c, 2), :, at : at + 64] = got[:, j]
+            return 0
+
+        lax.fori_loop(0, 4, attend, 0)
+        if head == 0:
+            gather_u.stage2()
+        if head == 1:
+            gather_d.stage2()
+    att_x.start()
+    gather_u.stage3()
+    gather_d.stage3()
+    gather_o.finish()
+    for w in range(4):
+        for k in range(2):
+            r.wout[:, :, k, :, 192 * w : 192 * w + 192] = r.go[w, :, :, :, 192 * k : 192 * k + 192]
+    for v in range(2):
+        rows = pl.ds(128 * v, 128)
+        r.gy[rows] = (d_out[rows].astype(F32) * live[v].astype(F32)).astype(BF16)
+    r.turned[...] = turned(r.gy[...])
+    att_x.wait()
+    for v in range(2):
+        for group in range(4):
+            for j in range(2):
+                row = 128 * v + 64 * j
+                r.att[row : row + 64, 192 * group : 192 * group + 192] = r.at[4 * v + group, :, 192 * j : 192 * j + 192]
+    mid = x[...].astype(F32) + dot(r.att[...], r.wout[...].reshape(768, 768))
+    r.y[...] = mid
+    hat, rstd = norm_stats(mid)
+    r.hat_b[...] = hat
+    r.rstd_b[...] = rstd
+    hidden = hat * r.gains[16:17] + r.gains[24:25]
+    r.h[...] = hidden.astype(BF16)
+    r.turned_b[...] = turned(hidden)
+    r.back[...] = jnp.zeros((256, 768), F32)
+    gather_p.stage4()
+    gather_u.finish()
+    gather_d.finish()
+    gather_p.finish()
+    for g in (*gathers, gather_p):
+        g.drain()
+
+    def feed(f, _):
+        w_up_f = rows_of(r.gu, f, 768)
+        up = dot(r.h[...], w_up_f)
+        square = up * up
+        bend = jnp.tanh(GELU_C * (up + 0.044715 * up * square))
+        act = (0.5 * up * (1.0 + bend)).astype(BF16)
+        slope = 0.5 * (1.0 + bend) + 0.5 * up * (1.0 - bend * bend) * (GELU_C * (1.0 + 0.134145 * square))
+        grads = []
+        for k in range(2):
+            w_down_f = rows_of(r.gd, (f, k), 768)
+            act_k = act[:, 384 * k : 384 * k + 384]
+            r.y[...] += dot_nt(act_k, w_down_f)
+            grads.append((dot(r.gy[...], w_down_f) * slope[:, 384 * k : 384 * k + 384]).astype(BF16))
+            r.gd[f, k] = dot(r.turned[...], act_k).astype(BF16).reshape(4, 192, 384)
+        grad_up = jnp.concatenate(grads, axis=1)
+        r.back[...] += dot_nt(grad_up, w_up_f)
+        r.gu[f] = dot(r.turned_b[...], grad_up).astype(BF16).reshape(4, 2, 96, 768)
+        return 0
+
+    lax.fori_loop(0, 4, feed, 0)
+    scatter_p.stage_c()
+    scatter_d.stage_c()
+    scatter_u.stage_c()
+    output[...] = r.y[...].astype(BF16)
+
+    grad_h = r.back[...]
+    r.rn[...] = jnp.zeros((4, 4, 2, 8, 128), F32)
+
+    def put_norm(w, row):
+        for s in range(8):
+            r.rn[w, s // 2, s % 2, 0:1, 0:96] = row[:, 96 * s : 96 * s + 96]
+
+    put_norm(2, jnp.sum(grad_h * r.hat_b[...], axis=0, keepdims=True))
+    put_norm(3, jnp.sum(grad_h, axis=0, keepdims=True))
+    mid_grad = norm_back(grad_h, r.hat_b[...], r.rstd_b[...], r.gains[16:17])
+    for v in range(2):
+        rows = slice(128 * v, 128 * v + 128)
+        r.mid_grad[rows] = mid_grad[rows] + d_out[rows].astype(F32) * live[v].astype(F32)
+    r.h[...] = r.mid_grad[...].astype(BF16)
+    att_x.drain()
+    grad_o = dot_nt(r.h[...], r.wout[...].reshape(768, 768)).astype(BF16)
+    for v in range(2):
+        for group in range(4):
+            for j in range(2):
+                row = 128 * v + 64 * j
+                r.ab[4 * v + group, :, 192 * j : 192 * j + 192] = grad_o[row : row + 64, 192 * group : 192 * group + 192]
+    gro_x.start()
+    scatter_p.stage_z()
+    scatter_d.stage_d()
+    scatter_u.stage_d()
+    r.turned[...] = turned(r.att[...])
+    for w in range(4):
+        raw = dot(r.turned[...], r.h[:, 192 * w : 192 * w + 192]).astype(BF16).reshape(4, 2, 2, 48, 192)
+        for k in range(2):
+            r.go[w, :, :, :, 192 * k : 192 * k + 192] = raw[:, :, k]
+    scatter_o.stage_c()
+    qkv_x.drain()
+    gro_x.wait()
+
+    for head in range(3):
+        r.gk[...] = jnp.zeros((64, 1024), F32)
+        r.gv[...] = jnp.zeros((64, 1024), F32)
+
+        def attend_back(c, _, head=head):
+            q0 = pl.multiple_of(c * 256, 256)
+            halves = []
+            for j in range(2):
+                at = 192 * j + 64 * head
+                halves.append(r.gor[pl.ds(2 * c, 2), :, at : at + 64].reshape(2, 1, 64, 64))
+            grad = jnp.concatenate(halves, axis=1).reshape(256, 64)
+            prob = r.prob[head, pl.ds(q0, 256)]
+            grad_p = dot_nt(grad, r.vh[head])
+            prob_f = prob.astype(F32)
+            inner = jnp.sum(prob_f * grad_p, axis=-1, keepdims=True)
+            grad_s = (prob_f * (grad_p - inner)).astype(BF16)
+            grad_q = (dot(grad_s, r.kh[head]) * (1.0 / math.sqrt(HD))).astype(BF16).reshape(2, 2, 64, 64)
+            for j in range(2):
+                at = 576 * j + 64 * head
+                r.sb[pl.ds(2 * c, 2), :, at : at + 64] = grad_q[:, j]
+            r.gk[...] += dot_tn(r.qh[head, pl.ds(q0, 256)], grad_s)
+            r.gv[...] += dot_tn(grad, prob)
+            return 0
+
+        lax.fori_loop(0, 4, attend_back, 0)
+        for kind, grad in ((1, r.gk[...] * (1.0 / math.sqrt(HD))), (2, r.gv[...])):
+            grad = jnp.transpose(grad).astype(BF16).reshape(8, 2, 64, 64)
+            for j in range(2):
+                at = 576 * j + 192 * kind + 64 * head
+                r.sb[:, :, at : at + 64] = grad[:, j]
+        if head == 0:
+            scatter_d.stage_e()
+        if head == 1:
+            scatter_u.stage_e()
+    gqkv_x.start()
+    scatter_o.stage_d()
+    scatter_p.stage_d()
+    scatter_d.stage_f()
+    scatter_u.stage_f()
+    hidden = r.hat_a[...] * r.gains[0:1] + r.gains[8:9]
+    r.turned[...] = turned(hidden)
+    r.back[...] = jnp.zeros((256, 768), F32)
+    gqkv_x.wait()
+    for v in range(2):
+        for group in range(4):
+            for kind in range(3):
+                for j in range(2):
+                    row, at = 128 * v + 64 * j, 576 * j + 192 * kind
+                    to = 768 * kind + 192 * group
+                    r.wide[row : row + 64, to : to + 192] = r.gb[4 * v + group, :, at : at + 192]
+    for w in range(4):
+        grad = r.wide[:, 576 * w : 576 * w + 576]
+        r.back[...] += dot_nt(grad, rows_of(r.gq, w, 768))
+        r.gq[w] = dot(r.turned[...], grad).astype(BF16).reshape(4, 2, 96, 576)
+    scatter_q.stage_c()
+    scatter_r.stage_c()
+    grad_h = r.back[...]
+    put_norm(0, jnp.sum(grad_h * r.hat_a[...], axis=0, keepdims=True))
+    put_norm(1, jnp.sum(grad_h, axis=0, keepdims=True))
+    scatter_n.stage_c()
+    scatter_q.stage_d()
+    scatter_r.stage_d()
+    scatter_n.stage_d()
+    scatter_o.stage_e()
+    scatter_p.stage_e()
+    d_input[...] = r.mid_grad[...] + norm_back(grad_h, r.hat_a[...], r.rstd_a[...], r.gains[0:1])
+    red_d[0:96] = scatter_d.finish()
+    red_u[...] = scatter_u.finish()
+    red_d[96:192] = scatter_p.finish()
+    scatter_o.stage_f()
+    scatter_q.stage_e()
+    scatter_n.stage_e()
+    scatter_r.stage_e()
+    scatter_q.stage_f()
+    scatter_n.stage_f()
+    scatter_r.stage_f()
+    red_o[...] = scatter_o.finish()
+    red_q[0:48] = scatter_q.finish()
+    red_n[...] = scatter_n.finish()
+    red_q[48:96] = scatter_r.finish()
+    local = jnp.zeros((8, 128), F32)
+    for ref in (red_q, red_o, red_u, red_d, red_n):
+        local = local + jnp.sum(ref[...] * ref[...])
+    r.square[...] = local
+    r.squares[0] = local
+
+    def share(k):
+        to = ((p.w + k // 8) % 4, (p.s + k % 8) % 8)
+        return remote(r.square, r.squares.at[k], r.sum_sems, k, to)
+
+    def share_start(k, _):
+        share(k).start()
+        return 0
+
+    def share_wait(k, _):
+        share(k).wait()
+        return 0
+
+    lax.fori_loop(1, 32, share_start, 0)
+    for part in (count_x, gro_x, gqkv_x, *scatters, scatter_p):
+        part.drain()
+    lax.fori_loop(1, 32, share_wait, 0)
+    total[...] = jnp.sum(r.squares[...], axis=0)
+
+
+def adam_kernel(*refs):
+    passed, state, outs = refs[0:2], refs[2:23], refs[23:46]
+    here, sems = refs[46:67], refs[67]
+    through = [pltpu.make_async_copy(a, b, sems.at[21 + k]) for k, (a, b) in enumerate(zip(passed, outs[21:23]))]
+    loads = [pltpu.make_async_copy(a, b, sems.at[k]) for k, (a, b) in enumerate(zip(state, here))]
+    for copy in (*loads, *through):
+        copy.start()
+    fix_one = 1.0 - beta_one**STEP
+    fix_two = 1.0 - beta_two**STEP
+    rates = (rate_matrix, rate_output, rate_matrix, rate_matrix, rate_norm)
+    loads[20].wait()
+    norm = jnp.sqrt(here[20][0:1, 0:1])
+    factor = 1.0 / jnp.maximum(norm, 1.0)
+    outs[20][...] = norm
+    for k in range(5):
+        for part in range(4):
+            loads[5 * part + k].wait()
+        raw = here[k][...]
+        if k == 1:
+            raw = jnp.concatenate([raw[:, 0:192], raw[:, 192:384]], axis=0)
+        if k == 4:
+            raw = raw[0:1, 0:96]
+        grad = raw * factor
+        weight = here[5 + k][...]
+        first = beta_one * here[10 + k][...] + (1.0 - beta_one) * grad
+        second = beta_two * here[15 + k][...] + (1.0 - beta_two) * grad * grad
+        stride = first / fix_one / (jnp.sqrt(second / fix_two) + adam_eps)
+        decay = 0.0 if k == 4 else decay_rate
+        outs[k][...] = grad
+        outs[5 + k][...] = weight - rates[k] * (stride + decay * weight)
+        outs[10 + k][...] = first
+        outs[15 + k][...] = second
+    for copy in through:
+        copy.wait()
+
+
+def fused_device(
+    layer_input, d_out, rand_ids, live_mask, w_qkv, w_out, w_up, w_down, norm_params,
+    m_qkv, m_out, m_up, m_down, m_norm, v_qkv, v_out, v_up, v_down, v_norm,
+):
+    vmem, smem, anywhere = (pl.BlockSpec(memory_space=kind) for kind in (pltpu.VMEM, pltpu.SMEM, pl.ANY))
+    ids = rand_ids.transpose(0, 2, 3, 1).reshape(24, 6)
+    leaves, tree = jax.tree.flatten(scratch())
+    reduced = [(96, 576), (48, 384), (96, 768), (192, 384), (8, 128), (8, 128)]
+    shape = jax.ShapeDtypeStruct
+    output, d_input, *grads, total = pl.pallas_call(
+        functools.partial(kernel, tree),
+        out_shape=[shape((256, 768), BF16), shape((256, 768), F32)] + [shape(dims, F32) for dims in reduced],
+        in_specs=[smem, smem] + [vmem] * 7,
+        out_specs=[vmem] * 8,
+        scratch_shapes=leaves,
+        compiler_params=pltpu.CompilerParams(collective_id=0, has_side_effects=True, vmem_limit_bytes=VMEM_LIMIT),
+    )(
+        live_mask, ids, layer_input.reshape(256, 768), d_out.reshape(256, 768), w_qkv, w_out, w_up, w_down.T,
+        norm_params.reshape(1, 96),
+    )
+    state = (
+        *grads,
+        w_qkv, w_out, w_up, w_down.T, norm_params.reshape(1, 96),
+        m_qkv, m_out, m_up, m_down.T, m_norm.reshape(1, 96),
+        v_qkv, v_out, v_up, v_down.T, v_norm.reshape(1, 96),
+        total,
+    )
+    made = pl.pallas_call(
+        adam_kernel,
+        out_shape=[shape(w.shape, F32) for w in state[5:10]] * 4
+        + [shape((1, 1), F32), shape(output.shape, BF16), shape(d_input.shape, F32)],
+        in_specs=[anywhere] * 23,
+        out_specs=[vmem] * 23,
+        scratch_shapes=[pltpu.VMEM(a.shape, F32) for a in state] + [pltpu.SemaphoreType.DMA((23,))],
+        compiler_params=pltpu.CompilerParams(vmem_limit_bytes=VMEM_LIMIT),
+    )(output, d_input, *state)
+    updated = [m.T if k % 5 == 3 else m.reshape(-1) if k % 5 == 4 else m for k, m in enumerate(made[:20])]
+    return (made[21].reshape(2, 128, 768), made[22].reshape(2, 128, 768), *updated, made[20].reshape(1))
+
+
 def solution(mesh):
     placed = (
         P("win", "seq", None),
@@ -244,8 +1122,9 @@
         P("seq", "win"),
         P(("win", "seq")),
     )
+    fused = mesh.shape["win"] == 4 and mesh.shape["seq"] == 8
     return jax.shard_map(
-        per_device,
+        fused_device if fused else per_device,
         mesh=mesh,
         in_specs=placed,
         out_specs=(

time: 690 us -> 220 us (0.32); the launches traced: 681 us -> 219 us
  waiting for transfers between devices: 286 us -> 0 us
  Pallas kernels: 0 us -> 217 us
  blocking collectives: 185 us -> 0 us
  matrix products: 78.7 us -> 0 us
  local copies, waits for them, and re-layouts: 69 us -> 1.46 us
  other arithmetic: 41.1 us -> 0 us
  between operations: 19.9 us -> 0.84 us
    pallas_call x0 -> x2, Pallas kernels: none -> 217 us  [the longest x1 211 us: fused_device(): pl.pallas_call(functools.partial(kernel, tree), out_shape=[shape((256, 76...]
    reduce_scatter x5 -> x0, waiting for transfers between devices: 139 us -> none  [the longest x4 117 us: per_device(): lax.psum_scatter(raw.astype(jnp.bfloat16), 'seq', scatter_dimension=0, ti...]
    unnamed x2 -> x0, blocking collectives: 79.3 us -> none
    unnamed x18 -> x0, waiting for transfers between devices: 78.1 us -> none
    all_gather x5 -> x0, waiting for transfers between devices: 69.5 us -> none  [the longest x4 45.8 us: per_device(): lax.all_gather(lax.all_gather(low, 'win', axis=1, tiled=True), 'seq', axi...]
    dot_general x16 -> x0, matrix products: 68.8 us -> none  [the longest x1 7.75 us: per_device(): up_proj = jnp.dot(h_two, full_up, preferred_element_type=jnp.float32)]
    all_gather x4 -> x0, blocking collectives: 64.6 us -> none  [per_device(): lax.all_gather(low, 'win', axis=1, tiled=True)]
    unnamed x89 -> x2, local copies, waits for them, and re-layouts: 52.3 us -> 0.68 us
  transfers between devices with their start and end apart: 14 -> 0, of which waited for: 10 -> 0; matrix products, arithmetic and copies ran while one was open for 23% -> 0% of each run, Pallas kernels for 0% -> 0%
where the time goes in v2:
time: 220 us; the launch traced here: 219 us
  Pallas kernels  217 us (99%)
    pallas_call x1, Pallas kernels, fused_device(): pl.pallas_call(functools.partial(kernel, tree), out_shape=[shape((256, 76...  211 us
    pallas_call x1, Pallas kernels, fused_device(): pl.pallas_call(adam_kernel, out_shape=[shape(w.shape, F32) for w in state...  5.75 us

profile of v2, /device:TPU:0, one launch (start us, length us, event | category | flops | bytes accessed | tf_op | source)
XLA Modules:
  0.0 219.3 jit_solution(3784376841352381620)
XLA Ops:
  0.7 0.0 copy-start
  0.7 0.7 copy-done
  1.4 0.1 reshape.86
  1.4 0.7 copy.44.rand_ids
  2.1 211.3 %shard_map.362 = (bf16[256,768]{1,0:T(8,128)(2,1)}, f32[256,768]{1,0:T(8,128)}, f32[96,576]{1,0:T(8,128)}, f32[48,384]{1,0:T(8,128)}, f32[96,768]{1,0:T(8,128)},...) custom-call(s32[2]{0:T(128)} %live.1, s32[24,6]{1,0:T(8,128)} %copy.44.rand_ids, ...), custom_call_target="tpu_custom_call" | custom-call | tf_op jit(solution)/shard_map/pallas_call | solution.py:1072
  213.4 5.8 %shard_map.363 = (f32[96,576]{1,0:T(8,128)}, f32[96,192]{1,0:T(8,128)}, f32[96,768]{1,0:T(8,128)}, f32[192,384]{1,0:T(8,128)}, f32[1,96]{1,0:T(1,128)}, /*index=...) custom-call(bf16[256,768]{1,0:T(8,128)(2,1)} %get-tuple-element.54.r, ...), custom_call_target="tpu_custom_call" | custom-call | tf_op jit(solution)/shard_map/pallas_call | solution.py:1090
  (1 shorter events, 0.0 us)
Async XLA Ops:
  0.7 0.7 copy-start

commit v3 on v2

--- a/solution.py
+++ b/solution.py
@@ -267,6 +267,18 @@
         self.par = s + self.turn
         self.roles = (s, self.n1, self.n2, self.nd)
         self.par_roles = tuple(r + self.turn for r in (s, self.n2, self.n1, self.nd))
+        self.x, self.y = x, y
+        self.mate = (self.w + 1 - 2 * (self.w % 2), s)
+
+    def chip(self, k):
+        x = self.x + (1 - k % 2) * (1 - 2 * self.x)
+        y = self.y + (1 - k // 2) * (1 - 2 * self.y)
+        return 2 * y + x
+
+    def role_for_partner(self, chip):
+        dx = (chip % 2 - self.x) * (chip % 2 - self.x)
+        dy = (chip // 2 - self.y) * (chip // 2 - self.y)
+        return self.c * (dx + 2 * dy) + (1 - self.c) * (dy + 2 * dx)
 
 
 class Blocks:
@@ -283,13 +295,10 @@
         every = slice(None)
         return self.buf.at[(s // 2, s % 2, every, self.rows) if self.seq_first else (every, s // 2, s % 2, self.rows)]
 
-    def core(self, c, w=slice(None)):
-        return self.buf.at[:, c, w, self.rows]
-
 
 class Gather:
-    def __init__(self, place, blocks, sems):
-        self.p, self.b, self.sems = place, blocks, sems
+    def __init__(self, place, blocks, sems, staged=None):
+        self.p, self.b, self.sems, self.staged = place, blocks, sems, staged
 
     def push(self, s, k, to):
         remote(self.b.group(s), self.b.group(s), self.sems, k, (self.p.w, to)).start()
@@ -298,8 +307,9 @@
         remote(self.b.group(s), self.b.group(s), self.sems, k, (self.p.w, self.p.par)).wait_recv()
 
     def along(self, dz, w):
-        block = self.b.block(w, self.p.s)
-        return remote(block, block, self.sems, dz - 1, ((self.p.w + dz) % 4, self.p.s))
+        p, block = self.p, self.b.block(w, self.p.s)
+        source = block if self.staged is None else self.staged.at[(p.w + dz) % 2, self.b.rows]
+        return remote(source, block, self.sems, dz - 1, ((p.w + dz) % 4, p.s))
 
     def z_send(self):
         for dz in (1, 2, 3):
@@ -338,57 +348,6 @@
             remote(self.b.group(s), self.b.group(s), self.sems, k, (p.w, p.par)).wait_send()
 
 
-class PlaneGather:
-    def __init__(self, place, blocks, sems):
-        self.p, self.b, self.sems = place, blocks, sems
-
-    def one(self, s, k, to):
-        return remote(self.b.block(self.p.w, s), self.b.block(self.p.w, s), self.sems, k, (self.p.w, to))
-
-    def layer(self, c, w, k, dev):
-        return remote(self.b.core(c, w), self.b.core(c, w), self.sems, k, dev)
-
-    def stage1(self):
-        p = self.p
-        self.one(p.s, 3, p.n1).start()
-        self.one(p.s, 4, p.n2).start()
-
-    def stage2(self):
-        p = self.p
-        self.one(p.n1, 3, p.n1).wait_recv()
-        self.one(p.n1, 5, p.n2).start()
-
-    def stage3(self):
-        p = self.p
-        self.one(p.n2, 4, p.n2).wait_recv()
-        self.one(p.nd, 5, p.n2).wait_recv()
-        for dz in (1, 2, 3):
-            self.layer(p.c, p.w, dz - 1, ((p.w + dz) % 4, p.s)).start()
-        self.layer(p.c, p.w, 6, (p.w, p.par)).start()
-
-    def stage4(self):
-        p = self.p
-        for dz in (1, 2, 3):
-            w = (p.w + 4 - dz) % 4
-            self.layer(p.c, w, dz - 1, (w, p.s)).wait_recv()
-            self.layer(p.c, w, 6 + dz, (p.w, p.par)).start()
-
-    def finish(self):
-        p = self.p
-        for dz in range(4):
-            self.layer(1 - p.c, (p.w + 4 - dz) % 4, 6 + dz, (p.w, p.par)).wait_recv()
-
-    def drain(self):
-        p = self.p
-        self.one(p.s, 3, p.n1).wait_send()
-        self.one(p.s, 4, p.n2).wait_send()
-        self.one(p.n1, 5, p.n2).wait_send()
-        for dz in (1, 2, 3):
-            self.layer(p.c, p.w, dz - 1, ((p.w + dz) % 4, p.s)).wait_send()
-        for dz in range(4):
-            self.layer(p.c, (p.w + 4 - dz) % 4, 6 + dz, (p.w, p.par)).wait_send()
-
-
 class Scatter:
     def __init__(self, place, blocks, space, sems):
         self.p, self.b, self.sems = place, blocks, sems
@@ -416,6 +375,11 @@
     def stage_c(self):
         for copy in self.copies_c():
             copy.start()
+
+    def stage_c_of(self, chip):
+        p = self.p
+        role = p.role_for_partner(chip)
+        remote(self.b.group(2 * chip + 1 - p.c), self.c.at[role], self.sems, role, (p.w, p.par)).start()
 
     def stage_d(self):
         waits, sends = self.copies_c(), self.copies_d()
@@ -449,71 +413,17 @@
             total = total + self.f[k].astype(F32)
         return total
 
+    def finish_halves(self):
+        p = self.p
+        for copy in self.copies_f():
+            copy.wait_recv()
+        alike = self.c[0, p.w].astype(F32) + self.f[1].astype(F32)
+        other = self.f[0].astype(F32) + self.f[2].astype(F32)
+        even = p.w % 2 == 0
+        return jnp.where(even, alike, other), jnp.where(even, other, alike)
+
     def drain(self):
         for copy in (*self.copies_c(), *self.copies_d(), self.copy_e(), *self.copies_f()):
-            copy.wait_send()
-
-
-class PlaneScatter:
-    def __init__(self, place, blocks, space, sems):
-        self.p, self.b, self.sems = place, blocks, sems
-        self.c, self.z, self.d, self.e = space
-
-    def copy_c(self):
-        p = self.p
-        return remote(self.b.core(1 - p.c), self.c, self.sems, 0, (p.w, p.par))
-
-    def copies_z(self):
-        p = self.p
-        return [
-            remote(self.c.at[:, (p.w + dz) % 4], self.z.at[dz - 1], self.sems, dz, ((p.w + dz) % 4, p.s)) for dz in (1, 2, 3)
-        ]
-
-    def copies_d(self):
-        p = self.p
-        return [remote(self.c.at[r // 2, p.w], self.d.at[k], self.sems, 4 + k, (p.w, p.n2)) for k, r in enumerate((p.n2, p.nd))]
-
-    def copy_e(self):
-        p = self.p
-        return remote(self.c.at[p.n1 // 2, p.w], self.e, self.sems, 6, (p.w, p.n1))
-
-    def stage_c(self):
-        self.copy_c().start()
-
-    def stage_z(self):
-        p = self.p
-        self.copy_c().wait_recv()
-        for w in range(4):
-            for chip in range(4):
-                self.c[chip, w] = self.c[chip, w] + self.b.read(w, 2 * chip + p.c)
-        for copy in self.copies_z():
-            copy.start()
-
-    def stage_d(self):
-        p = self.p
-        for k, copy in enumerate(self.copies_z()):
-            copy.wait_recv()
-            for chip in range(4):
-                self.c[chip, p.w] = self.c[chip, p.w] + self.z[k, chip]
-        for copy in self.copies_d():
-            copy.start()
-
-    def stage_e(self):
-        p = self.p
-        waits = self.copies_d()
-        for k, r in ((1, p.n1), (0, p.s)):
-            waits[k].wait_recv()
-            self.c[r // 2, p.w] = self.c[r // 2, p.w] + self.d[k]
-            if k == 1:
-                self.copy_e().start()
-
-    def finish(self):
-        p = self.p
-        self.copy_e().wait_recv()
-        return self.c[p.s // 2, p.w].astype(F32) + self.e[...].astype(F32)
-
-    def drain(self):
-        for copy in (self.copy_c(), *self.copies_z(), *self.copies_d(), self.copy_e()):
             copy.wait_send()
 
 
@@ -566,6 +476,14 @@
 
 def turned(value):
     return jnp.transpose(value.astype(F32)).astype(BF16)
+
+
+GIVEN = (
+    ((256, 768), BF16), ((256, 768), BF16), ((96, 576), F32), ((96, 192), F32), ((96, 768), F32), ((192, 384), F32), ((1, 96), F32),
+)
+KEPT = (
+    ((256, 768), BF16), ((256, 768), F32), ((96, 576), F32), ((48, 384), F32), ((96, 768), F32), ((192, 384), F32), ((8, 128), F32), ((8, 128), F32),
+)
 
 
 class Space(NamedTuple):
@@ -577,11 +495,12 @@
     rn: Any
     sn: Any
     sq: Any
-    sr: Any
     so: Any
     su: Any
     sd: Any
-    sp: Any
+    half_u: Any
+    half_d: Any
+    wd: Any
     gather_sems: Any
     scatter_sems: Any
     exchange_sems: Any
@@ -602,22 +521,35 @@
     att: Any
     wout: Any
     turned: Any
-    turned_b: Any
+    turned_h: Any
+    turned_g: Any
     gains: Any
     hat_a: Any
     hat_b: Any
     rstd_a: Any
     rstd_b: Any
     h: Any
+    hb: Any
+    hs: Any
+    gys: Any
+    back_out: Any
+    back_in: Any
+    y_out: Any
+    y_in: Any
+    mate_sems: Any
     wide: Any
     y: Any
-    gy: Any
     back: Any
     mid_grad: Any
     gk: Any
     gv: Any
+    act: Any
+    slope: Any
     square: Any
     squares: Any
+    given: Any
+    kept: Any
+    io_sems: Any
 
 
 def scratch():
@@ -627,25 +559,25 @@
     def sems(count):
         return (pltpu.SemaphoreType.DMA((count,)),) * 2
 
-    half = (96, 384)
-    rows, wide = (256, 768), (8, 64, 1152)
+    rows, wide = (256, 768), (3, 8, 64, 384)
     return Space(
         gn=pltpu.VMEM((4, 4, 2, 8, 128), F32),
         gq=pltpu.VMEM((4, 4, 2, 96, 576), BF16),
         go=pltpu.VMEM((4, 4, 2, 48, 384), BF16),
-        gu=pltpu.VMEM((4, 4, 2, 96, 768), BF16),
-        gd=pltpu.VMEM((4, 2, 4, 192, 384), BF16),
+        gu=pltpu.VMEM((4, 4, 2, 96, 384), BF16),
+        gd=pltpu.VMEM((4, 2, 4, 96, 384), BF16),
         rn=pltpu.VMEM((4, 4, 2, 8, 128), F32),
         sn=scatter(8, 128, kind=F32),
-        sq=scatter(48, 576),
-        sr=scatter(48, 576),
+        sq=tuple(scatter(32, 576) for _ in range(3)),
         so=scatter(48, 384),
-        su=scatter(96, 768),
-        sd=scatter(*half),
-        sp=tuple(pltpu.VMEM((*lead, *half), BF16) for lead in ((4, 4), (3, 4), (2,), ())),
-        gather_sems=tuple(sems(10) for _ in range(7)),
-        scatter_sems=tuple(sems(10) for _ in range(7)),
-        exchange_sems=tuple(sems(8) for _ in range(5)),
+        su=tuple(scatter(48, 384) for _ in range(2)),
+        sd=tuple(scatter(48, 384) for _ in range(2)),
+        half_u=pltpu.VMEM((2, 96, 384), BF16),
+        half_d=pltpu.VMEM((2, 96, 384), BF16),
+        wd=pltpu.VMEM((4, 4, 2, 96, 384), BF16),
+        gather_sems=tuple(sems(10) for _ in range(9)),
+        scatter_sems=tuple(sems(10) for _ in range(9)),
+        exchange_sems=tuple(sems(8) for _ in range(9)),
         sum_sems=sems(32),
         count_out=pltpu.VMEM((8, 8, 128), F32),
         counts=pltpu.VMEM((8, 8, 128), F32),
@@ -663,27 +595,46 @@
         att=pltpu.VMEM(rows, BF16),
         wout=pltpu.VMEM((4, 2, 2, 48, 768), BF16),
         turned=pltpu.VMEM((768, 256), BF16),
-        turned_b=pltpu.VMEM((768, 256), BF16),
+        turned_h=pltpu.VMEM((768, 512), BF16),
+        turned_g=pltpu.VMEM((768, 512), BF16),
         gains=pltpu.VMEM((32, 768), F32),
         hat_a=pltpu.VMEM(rows, F32),
         hat_b=pltpu.VMEM(rows, F32),
         rstd_a=pltpu.VMEM((256, 1), F32),
         rstd_b=pltpu.VMEM((256, 1), F32),
         h=pltpu.VMEM(rows, BF16),
+        hb=pltpu.VMEM(rows, BF16),
+        hs=pltpu.VMEM((2, *rows), BF16),
+        gys=pltpu.VMEM((2, *rows), BF16),
+        back_out=pltpu.VMEM(rows, BF16),
+        back_in=pltpu.VMEM(rows, BF16),
+        y_out=pltpu.VMEM(rows, BF16),
+        y_in=pltpu.VMEM(rows, BF16),
+        mate_sems=sems(4),
         wide=pltpu.VMEM((256, 2304), BF16),
-        y=pltpu.VMEM(rows, F32),
-        gy=pltpu.VMEM(rows, BF16),
-        back=pltpu.VMEM(rows, F32),
+        y=pltpu.VMEM((512, 768), F32),
+        back=pltpu.VMEM((512, 768), F32),
         mid_grad=pltpu.VMEM(rows, F32),
         gk=pltpu.VMEM((64, 1024), F32),
         gv=pltpu.VMEM((64, 1024), F32),
+        act=pltpu.VMEM((4, 512, 384), BF16),
+        slope=pltpu.VMEM((4, 512, 384), BF16),
         square=pltpu.VMEM((8, 128), F32),
         squares=pltpu.VMEM((32, 8, 128), F32),
-    )
-
-
-def kernel(tree, live, rand_ids, x, d_out, w_qkv, w_out, w_up, w_down, norm, output, d_input, red_q, red_o, red_u, red_d, red_n, total, *rest):
-    r = jax.tree.unflatten(tree, rest)
+        given=tuple(pltpu.VMEM(dims, kind) for dims, kind in GIVEN),
+        kept=tuple(pltpu.VMEM(dims, kind) for dims, kind in KEPT),
+        io_sems=pltpu.SemaphoreType.DMA((15,)),
+    )
+
+
+def kernel(tree, live, rand_ids, *refs):
+    r = jax.tree.unflatten(tree, refs[15:])
+    x, d_out, w_qkv, w_out, w_up, w_down, norm = r.given
+    output, d_input, red_q, red_o, red_u, red_d, red_n, total = r.kept
+    loads = [pltpu.make_async_copy(a, b, r.io_sems.at[k]) for k, (a, b) in enumerate(zip(refs[:7], r.given))]
+    stores = [pltpu.make_async_copy(a, b, r.io_sems.at[7 + k]) for k, (a, b) in enumerate(zip(r.kept, refs[7:15]))]
+    for k in (6, 2, 5, 3, 4, 0, 1):
+        loads[k].start()
     p = Place()
     barrier = pltpu.get_barrier_semaphore()
 
@@ -694,39 +645,41 @@
 
     lax.fori_loop(1, 32, greet, 0)
 
-    all_n, all_q, all_r = Blocks(r.gn), Blocks(r.gq, count=48), Blocks(r.gq, start=48, count=48)
-    all_o, all_u = Blocks(r.go), Blocks(r.gu)
-    all_d, all_p = Blocks(r.gd, True, count=96), Blocks(r.gd, True, start=96, count=96)
-    gathers = [Gather(p, b, m) for b, m in zip((all_n, all_q, all_r, all_o, all_u, all_d), r.gather_sems)]
-    gather_n, gather_q, gather_r, gather_o, gather_u, gather_d = gathers
-    gather_p = PlaneGather(p, all_p, r.gather_sems[6])
-    scatters = [
-        Scatter(p, b, space, m)
-        for b, space, m in zip(
-            (Blocks(r.rn), all_q, all_r, all_o, all_u, all_d), (r.sn, r.sq, r.sr, r.so, r.su, r.sd), r.scatter_sems
-        )
-    ]
-    scatter_n, scatter_q, scatter_r, scatter_o, scatter_u, scatter_d = scatters
-    scatter_p = PlaneScatter(p, all_p, r.sp, r.scatter_sems[6])
+    blocks_q = [Blocks(r.gq, start=32 * k, count=32) for k in range(3)]
+    blocks_u = [Blocks(r.gu, start=48 * k, count=48) for k in range(2)]
+    blocks_d = [Blocks(r.gd, True, start=48 * k, count=48) for k in range(2)]
+    every = (*blocks_q, Blocks(r.go), *blocks_u, *blocks_d)
+    staged = (None,) * 4 + (r.half_u,) * 2 + (r.half_d,) * 2
+    gathers = [Gather(p, Blocks(r.gn), r.gather_sems[8])]
+    gathers += [Gather(p, b, m, half) for b, m, half in zip(every, r.gather_sems, staged)]
+    gn, gq0, gq1, gq2, go, gu0, gu1, gd0, gd1 = gathers
+    scatters = [Scatter(p, Blocks(r.rn), r.sn, r.scatter_sems[8])]
+    scatters += [Scatter(p, b, space, m) for b, space, m in zip(every, (*r.sq, r.so, *r.su, *r.sd), r.scatter_sems)]
+    sn, sq0, sq1, sq2, so, su0, su1, sd0, sd1 = scatters
+    mate_h = remote(r.hs.at[0], r.hs.at[1], r.mate_sems, 0, p.mate)
+    mate_g = remote(r.gys.at[0], r.gys.at[1], r.mate_sems, 1, p.mate)
+    mate_back = remote(r.back_out, r.back_in, r.mate_sems, 2, p.mate)
+    mate_y = remote(r.y_out, r.y_in, r.mate_sems, 3, p.mate)
     count_x = Exchange(p, r.count_out, r.counts, r.exchange_sems[0])
-    qkv_x = Exchange(p, r.sb, r.rb, r.exchange_sems[1])
-    att_x = Exchange(p, r.ab, r.at, r.exchange_sems[2])
-    gro_x = Exchange(p, r.ab, r.gor, r.exchange_sems[3])
-    gqkv_x = Exchange(p, r.sb, r.gb, r.exchange_sems[4])
+    att_x = Exchange(p, r.ab, r.at, r.exchange_sems[1])
+    gro_x = Exchange(p, r.ab, r.gor, r.exchange_sems[2])
+    qkv_x = [Exchange(p, r.sb.at[h], r.rb.at[h], r.exchange_sems[3 + h]) for h in range(3)]
+    gqkv_x = [Exchange(p, r.sb.at[h], r.gb.at[h], r.exchange_sems[6 + h]) for h in range(3)]
     chip, core = p.s // 2, p.c
 
     r.gn[p.w, chip, core] = jnp.zeros((8, 128), F32)
+    loads[6].wait()
     r.gn[p.w, chip, core, 0:1, 0:96] = norm[...].astype(BF16).astype(F32)
+    loads[2].wait()
     r.gq[p.w, chip, core] = w_qkv[...].astype(BF16)
-    r.gd[chip, core, p.w] = w_down[...].astype(BF16)
     pl.semaphore_wait(barrier, 31)
-    gather_n.z_send()
-    gather_q.z_send()
-    gather_r.z_send()
-    gather_p.stage1()
+    gq0.z_send()
+    gn.z_send()
+    gq1.z_send()
+    gq2.z_send()
+    loads[3].wait()
     for k in range(2):
         r.go[p.w, chip, core, :, 192 * k : 192 * k + 192] = w_out[48 * k : 48 * k + 48].astype(BF16)
-    gather_o.z_send()
 
     lane = lax.broadcasted_iota(jnp.int32, (8, 128), 1)
     sub = lax.broadcasted_iota(jnp.int32, (8, 128), 0)
@@ -742,16 +695,28 @@
                     counts = counts + ((sub == row) & (lane == drawn)).astype(F32)
             r.count_out[4 * v + group] = counts
     count_x.start()
-    r.gu[p.w, chip, core] = w_up[...].astype(BF16)
-    gather_u.z_send()
-    gather_d.z_send()
-
+    loads[4].wait()
+    loads[5].wait()
+    for half in range(2):
+        for k in range(2):
+            at, row = slice(192 * k, 192 * k + 192), 96 * k
+            r.half_u[half, :, at] = w_up[:, 384 * k + 192 * half : 384 * k + 192 * half + 192].astype(BF16)
+            r.half_d[half, :, at] = w_down[row : row + 96, 192 * half : 192 * half + 192].astype(BF16)
+    r.gu[p.w, chip, core] = r.half_u[p.w % 2]
+    r.gd[chip, core, p.w] = r.half_d[p.w % 2]
+    gq0.stage1()
+    loads[0].wait()
     hat, rstd = norm_stats(x[...].astype(F32))
     r.hat_a[...] = hat
     r.rstd_a[...] = rstd
-    gather_n.stage1()
-    gather_p.stage2()
-    gather_q.stage1()
+    loads[1].wait()
+    for v in range(2):
+        rows = slice(128 * v, 128 * v + 128)
+        r.gys[0, rows] = (d_out[rows].astype(F32) * live[v].astype(F32)).astype(BF16)
+    gn.stage1()
+    gq1.stage1()
+    gq0.stage2()
+    go.z_send()
 
     count_x.wait()
     spread = (
@@ -765,11 +730,15 @@
             at = 2 * (src % 2)
             r.bias[head, src // 2, at : at + 2] = wide[row : row + 2]
 
-    gather_n.stage2()
-    gather_r.stage1()
-    gather_q.stage2()
-    gather_n.stage3()
-    gather_n.finish()
+    gu0.z_send()
+    gq2.stage1()
+    gn.stage2()
+    gq1.stage2()
+    gq0.stage3()
+    gn.stage3()
+    gq2.stage2()
+    gn.finish()
+    mate_g.start()
     lane = lax.broadcasted_iota(jnp.int32, (128, 768), 1)
     sub = lax.broadcasted_iota(jnp.int32, (128, 768), 0)
     gains = jnp.zeros((32, 768), F32)
@@ -778,12 +747,15 @@
         gains = gains + dot(r.gn[:, s // 2, s % 2].reshape(32, 128).astype(BF16), place)
     r.gains[...] = gains
     r.h[...] = (r.hat_a[...] * r.gains[0:1] + r.gains[8:9]).astype(BF16)
-    gather_r.stage2()
-    gather_o.stage1()
-    gather_q.stage3()
-    gather_r.stage3()
-    gather_q.finish()
-    gather_r.finish()
+    go.stage1()
+    gq1.stage3()
+    gq2.stage3()
+    gq0.finish()
+    gu0.stage1()
+    gd1.z_send()
+    gq1.finish()
+    gq2.finish()
+    go.stage2()
 
     for w in range(4):
         part = dot(r.h[...], rows_of(r.gq, w, 768)).astype(BF16)
@@ -791,23 +763,22 @@
             kind, group = divmod(3 * w + k, 4)
             for v in range(2):
                 for j in range(2):
-                    row, at = 128 * v + 64 * j, 576 * j + 192 * kind
-                    r.sb[4 * v + group, :, at : at + 192] = part[row : row + 64, 192 * k : 192 * k + 192]
-    qkv_x.start()
-    gather_u.stage1()
-    gather_p.stage3()
-    gather_o.stage2()
-    gather_o.stage3()
-    gather_d.stage1()
-    qkv_x.wait()
-    for src in range(8):
-        for head in range(3):
+                    for head in range(3):
+                        row, at, col = 128 * v + 64 * j, 192 * j + 64 * kind, 192 * k + 64 * head
+                        r.sb[head, 4 * v + group, :, at : at + 64] = part[row : row + 64, col : col + 64]
+    gu1.z_send()
+    qkv_x[0].start()
+    go.stage3()
+    qkv_x[1].start()
+    qkv_x[2].start()
+
+    for head in range(3):
+        qkv_x[head].wait()
+        for src in range(8):
             for kind, ref in enumerate((r.qh, r.kh, r.vh)):
                 for j in range(2):
-                    row, at = 128 * src + 64 * j, 576 * j + 192 * kind + 64 * head
-                    ref[head, row : row + 64] = r.rb[src, :, at : at + 64]
-
-    for head in range(3):
+                    row, at = 128 * src + 64 * j, 192 * j + 64 * kind
+                    ref[head, row : row + 64] = r.rb[head, src, :, at : at + 64]
 
         def attend(c, _, head=head):
             q0 = pl.multiple_of(c * 256, 256)
@@ -824,20 +795,20 @@
 
         lax.fori_loop(0, 4, attend, 0)
         if head == 0:
-            gather_u.stage2()
+            go.finish()
+            gd0.z_send()
         if head == 1:
-            gather_d.stage2()
+            gu1.stage1()
     att_x.start()
-    gather_u.stage3()
-    gather_d.stage3()
-    gather_o.finish()
+    gu0.stage2()
+    gu1.stage2()
     for w in range(4):
         for k in range(2):
             r.wout[:, :, k, :, 192 * w : 192 * w + 192] = r.go[w, :, :, :, 192 * k : 192 * k + 192]
-    for v in range(2):
-        rows = pl.ds(128 * v, 128)
-        r.gy[rows] = (d_out[rows].astype(F32) * live[v].astype(F32)).astype(BF16)
-    r.turned[...] = turned(r.gy[...])
+    gd0.stage1()
+    mate_g.wait_recv()
+    for k in range(2):
+        r.turned_g[:, 256 * k : 256 * k + 256] = turned(r.gys[k])
     att_x.wait()
     for v in range(2):
         for group in range(4):
@@ -845,79 +816,121 @@
                 row = 128 * v + 64 * j
                 r.att[row : row + 64, 192 * group : 192 * group + 192] = r.at[4 * v + group, :, 192 * j : 192 * j + 192]
     mid = x[...].astype(F32) + dot(r.att[...], r.wout[...].reshape(768, 768))
-    r.y[...] = mid
+    r.y[0:256] = mid
+    r.y[256:512] = jnp.zeros((256, 768), F32)
     hat, rstd = norm_stats(mid)
     r.hat_b[...] = hat
     r.rstd_b[...] = rstd
-    hidden = hat * r.gains[16:17] + r.gains[24:25]
-    r.h[...] = hidden.astype(BF16)
-    r.turned_b[...] = turned(hidden)
-    r.back[...] = jnp.zeros((256, 768), F32)
-    gather_p.stage4()
-    gather_u.finish()
-    gather_d.finish()
-    gather_p.finish()
-    for g in (*gathers, gather_p):
+    r.hs[0] = (hat * r.gains[16:17] + r.gains[24:25]).astype(BF16)
+    mate_h.start()
+    gd0.stage2()
+    gu1.stage3()
+    gd1.stage1()
+    gu0.stage3()
+    r.back[...] = jnp.zeros((512, 768), F32)
+    r.turned_h[:, 0:256] = turned(r.hs[0])
+    gu0.finish()
+    gu1.finish()
+
+    for k in range(2):
+        if k == 1:
+            gd0.stage3()
+            gd1.stage2()
+            gd0.finish()
+            mate_h.wait_recv()
+            gd1.stage3()
+            r.turned_h[:, 256:512] = turned(r.hs[1])
+
+        def feed_up(f, _, k=k):
+            up = dot(r.hs[k], rows_of(r.gu, f, 768))
+            square = up * up
+            bend = jnp.tanh(GELU_C * (up + 0.044715 * up * square))
+            slope = 0.5 * (1.0 + bend) + 0.5 * up * (1.0 - bend * bend) * (GELU_C * (1.0 + 0.134145 * square))
+            r.act[f, 256 * k : 256 * k + 256] = (0.5 * up * (1.0 + bend)).astype(BF16)
+            r.slope[f, 256 * k : 256 * k + 256] = slope.astype(BF16)
+            return 0
+
+        lax.fori_loop(0, 4, feed_up, 0)
+    gd1.finish()
+    for g in gathers:
         g.drain()
 
-    def feed(f, _):
-        w_up_f = rows_of(r.gu, f, 768)
-        up = dot(r.h[...], w_up_f)
-        square = up * up
-        bend = jnp.tanh(GELU_C * (up + 0.044715 * up * square))
-        act = (0.5 * up * (1.0 + bend)).astype(BF16)
-        slope = 0.5 * (1.0 + bend) + 0.5 * up * (1.0 - bend * bend) * (GELU_C * (1.0 + 0.134145 * square))
-        grads = []
-        for k in range(2):
-            w_down_f = rows_of(r.gd, (f, k), 768)
-            act_k = act[:, 384 * k : 384 * k + 384]
-            r.y[...] += dot_nt(act_k, w_down_f)
-            grads.append((dot(r.gy[...], w_down_f) * slope[:, 384 * k : 384 * k + 384]).astype(BF16))
-            r.gd[f, k] = dot(r.turned[...], act_k).astype(BF16).reshape(4, 192, 384)
-        grad_up = jnp.concatenate(grads, axis=1)
-        r.back[...] += dot_nt(grad_up, w_up_f)
-        r.gu[f] = dot(r.turned_b[...], grad_up).astype(BF16).reshape(4, 2, 96, 768)
+    def unpack(f, _):
+        for c in range(2):
+            for j in range(2):
+                r.wd[f, :, j, :, 192 * c : 192 * c + 192] = r.gd[f, c, :, :, 192 * j : 192 * j + 192]
         return 0
 
-    lax.fori_loop(0, 4, feed, 0)
-    scatter_p.stage_c()
-    scatter_d.stage_c()
-    scatter_u.stage_c()
-    output[...] = r.y[...].astype(BF16)
-
-    grad_h = r.back[...]
-    r.rn[...] = jnp.zeros((4, 4, 2, 8, 128), F32)
-
-    def put_norm(w, row):
-        for s in range(8):
-            r.rn[w, s // 2, s % 2, 0:1, 0:96] = row[:, 96 * s : 96 * s + 96]
-
-    put_norm(2, jnp.sum(grad_h * r.hat_b[...], axis=0, keepdims=True))
-    put_norm(3, jnp.sum(grad_h, axis=0, keepdims=True))
-    mid_grad = norm_back(grad_h, r.hat_b[...], r.rstd_b[...], r.gains[16:17])
+    lax.fori_loop(0, 4, unpack, 0)
+    for k in (1, 0):
+
+        def feed_back(f, _, k=k):
+            rows = slice(256 * k, 256 * k + 256)
+            grad_up = (dot(r.gys[k], rows_of(r.wd, f, 768)) * r.slope[f, rows].astype(F32)).astype(BF16)
+            r.slope[f, rows] = grad_up
+            r.back[rows] += dot_nt(grad_up, rows_of(r.gu, f, 768))
+            return 0
+
+        lax.fori_loop(0, 4, feed_back, 0)
+        if k == 1:
+            r.back_out[...] = r.back[256:512].astype(BF16)
+            mate_back.start()
+
+    def feed_raw(k, _):
+        f = p.chip(k)
+        act = r.act[f]
+        r.y[...] += dot_nt(act, rows_of(r.wd, f, 768))
+        raw_down = dot(r.turned_g[...], act).astype(BF16).reshape(4, 2, 96, 384)
+        for c in range(2):
+            for j in range(2):
+                r.gd[f, c, :, :, 192 * j : 192 * j + 192] = raw_down[:, j, :, 192 * c : 192 * c + 192]
+        sd0.stage_c_of(f)
+        sd1.stage_c_of(f)
+        r.gu[f] = dot(r.turned_h[...], r.slope[f]).astype(BF16).reshape(4, 2, 96, 384)
+        return 0
+
+    lax.fori_loop(0, 4, feed_raw, 0)
+    su0.stage_c()
+    sd0.stage_d()
+    r.y_out[...] = r.y[256:512].astype(BF16)
+    mate_back.wait_recv()
+    su0.stage_d()
+    sd0.stage_e()
+
+    r.back[0:256] += r.back_in[...].astype(F32)
+    mid_grad = norm_back(r.back[0:256], r.hat_b[...], r.rstd_b[...], r.gains[16:17])
     for v in range(2):
         rows = slice(128 * v, 128 * v + 128)
         r.mid_grad[rows] = mid_grad[rows] + d_out[rows].astype(F32) * live[v].astype(F32)
-    r.h[...] = r.mid_grad[...].astype(BF16)
+    r.hb[...] = r.mid_grad[...].astype(BF16)
     att_x.drain()
-    grad_o = dot_nt(r.h[...], r.wout[...].reshape(768, 768)).astype(BF16)
+    grad_o = dot_nt(r.hb[...], r.wout[...].reshape(768, 768)).astype(BF16)
     for v in range(2):
         for group in range(4):
             for j in range(2):
                 row = 128 * v + 64 * j
                 r.ab[4 * v + group, :, 192 * j : 192 * j + 192] = grad_o[row : row + 64, 192 * group : 192 * group + 192]
     gro_x.start()
-    scatter_p.stage_z()
-    scatter_d.stage_d()
-    scatter_u.stage_d()
+    sd1.stage_d()
+    r.rn[...] = jnp.zeros((4, 4, 2, 8, 128), F32)
+
+    def put_norm(w, row):
+        for s in range(8):
+            r.rn[w, s // 2, s % 2, 0:1, 0:96] = row[:, 96 * s : 96 * s + 96]
+
+    put_norm(2, jnp.sum(r.back[0:256] * r.hat_b[...], axis=0, keepdims=True))
+    put_norm(3, jnp.sum(r.back[0:256], axis=0, keepdims=True))
+    su1.stage_c()
     r.turned[...] = turned(r.att[...])
     for w in range(4):
-        raw = dot(r.turned[...], r.h[:, 192 * w : 192 * w + 192]).astype(BF16).reshape(4, 2, 2, 48, 192)
+        raw = dot(r.turned[...], r.hb[:, 192 * w : 192 * w + 192]).astype(BF16).reshape(4, 2, 2, 48, 192)
         for k in range(2):
             r.go[w, :, :, :, 192 * k : 192 * k + 192] = raw[:, :, k]
-    scatter_o.stage_c()
-    qkv_x.drain()
+    for exchange in qkv_x:
+        exchange.drain()
     gro_x.wait()
+    so.stage_c()
+    su0.stage_e()
 
     for head in range(3):
         r.gk[...] = jnp.zeros((64, 1024), F32)
@@ -937,8 +950,7 @@
             grad_s = (prob_f * (grad_p - inner)).astype(BF16)
             grad_q = (dot(grad_s, r.kh[head]) * (1.0 / math.sqrt(HD))).astype(BF16).reshape(2, 2, 64, 64)
             for j in range(2):
-                at = 576 * j + 64 * head
-                r.sb[pl.ds(2 * c, 2), :, at : at + 64] = grad_q[:, j]
+                r.sb[head, pl.ds(2 * c, 2), :, 192 * j : 192 * j + 64] = grad_q[:, j]
             r.gk[...] += dot_tn(r.qh[head, pl.ds(q0, 256)], grad_s)
             r.gv[...] += dot_tn(grad, prob)
             return 0
@@ -947,58 +959,90 @@
         for kind, grad in ((1, r.gk[...] * (1.0 / math.sqrt(HD))), (2, r.gv[...])):
             grad = jnp.transpose(grad).astype(BF16).reshape(8, 2, 64, 64)
             for j in range(2):
-                at = 576 * j + 192 * kind + 64 * head
-                r.sb[:, :, at : at + 64] = grad[:, j]
-        if head == 0:
-            scatter_d.stage_e()
+                at = 192 * j + 64 * kind
+                r.sb[head, :, :, at : at + 64] = grad[:, j]
         if head == 1:
-            scatter_u.stage_e()
-    gqkv_x.start()
-    scatter_o.stage_d()
-    scatter_p.stage_d()
-    scatter_d.stage_f()
-    scatter_u.stage_f()
+            mate_y.start()
+        if head == 2:
+            sd0.stage_f()
+        gqkv_x[head].start()
+    su0.stage_f()
     hidden = r.hat_a[...] * r.gains[0:1] + r.gains[8:9]
     r.turned[...] = turned(hidden)
-    r.back[...] = jnp.zeros((256, 768), F32)
-    gqkv_x.wait()
-    for v in range(2):
-        for group in range(4):
-            for kind in range(3):
-                for j in range(2):
-                    row, at = 128 * v + 64 * j, 576 * j + 192 * kind
-                    to = 768 * kind + 192 * group
-                    r.wide[row : row + 64, to : to + 192] = r.gb[4 * v + group, :, at : at + 192]
+    r.back[0:256] = jnp.zeros((256, 768), F32)
+    for head in range(3):
+        gqkv_x[head].wait()
+        for v in range(2):
+            for group in range(4):
+                for kind in range(3):
+                    for j in range(2):
+                        row, at, to = 128 * v + 64 * j, 192 * j + 64 * kind, 768 * kind + 192 * group + 64 * head
+                        r.wide[row : row + 64, to : to + 64] = r.gb[head, 4 * v + group, :, at : at + 64]
+        if head == 0:
+            so.stage_d()
+            su1.stage_d()
+        if head == 1:
+            sd1.stage_e()
     for w in range(4):
         grad = r.wide[:, 576 * w : 576 * w + 576]
-        r.back[...] += dot_nt(grad, rows_of(r.gq, w, 768))
+        r.back[0:256] += dot_nt(grad, rows_of(r.gq, w, 768))
         r.gq[w] = dot(r.turned[...], grad).astype(BF16).reshape(4, 2, 96, 576)
-    scatter_q.stage_c()
-    scatter_r.stage_c()
-    grad_h = r.back[...]
+    sd1.stage_f()
+    sq2.stage_c()
+    sq1.stage_c()
+
+    def put_down(k, halves):
+        for half, value in enumerate(halves):
+            for j in range(2):
+                row, at = 96 * j + 48 * k, 192 * half
+                red_d[row : row + 48, at : at + 192] = value[:, 192 * j : 192 * j + 192]
+
+    def put_up(k, halves):
+        for half, value in enumerate(halves):
+            for j in range(2):
+                at = 384 * j + 192 * half
+                red_u[48 * k : 48 * k + 48, at : at + 192] = value[:, 192 * j : 192 * j + 192]
+
+    put_down(0, sd0.finish_halves())
+    so.stage_e()
+    su1.stage_e()
+    grad_h = r.back[0:256]
     put_norm(0, jnp.sum(grad_h * r.hat_a[...], axis=0, keepdims=True))
     put_norm(1, jnp.sum(grad_h, axis=0, keepdims=True))
-    scatter_n.stage_c()
-    scatter_q.stage_d()
-    scatter_r.stage_d()
-    scatter_n.stage_d()
-    scatter_o.stage_e()
-    scatter_p.stage_e()
+    put_down(1, sd1.finish_halves())
+    stores[5].start()
+    sq2.stage_d()
+    sq1.stage_d()
+    sq0.stage_c()
+    sq0.stage_d()
+    so.stage_f()
+    sq2.stage_e()
+    sq1.stage_e()
+    su1.stage_f()
+    sn.stage_c()
     d_input[...] = r.mid_grad[...] + norm_back(grad_h, r.hat_a[...], r.rstd_a[...], r.gains[0:1])
-    red_d[0:96] = scatter_d.finish()
-    red_u[...] = scatter_u.finish()
-    red_d[96:192] = scatter_p.finish()
-    scatter_o.stage_f()
-    scatter_q.stage_e()
-    scatter_n.stage_e()
-    scatter_r.stage_e()
-    scatter_q.stage_f()
-    scatter_n.stage_f()
-    scatter_r.stage_f()
-    red_o[...] = scatter_o.finish()
-    red_q[0:48] = scatter_q.finish()
-    red_n[...] = scatter_n.finish()
-    red_q[48:96] = scatter_r.finish()
+    stores[1].start()
+    sn.stage_d()
+    red_o[...] = so.finish()
+    stores[3].start()
+    mate_y.wait_recv()
+    output[...] = (r.y[0:256] + r.y_in[...].astype(F32)).astype(BF16)
+    stores[0].start()
+    sq2.stage_f()
+    sq1.stage_f()
+    sq0.stage_e()
+    sn.stage_e()
+    sq0.stage_f()
+    sn.stage_f()
+    put_up(1, su1.finish_halves())
+    put_up(0, su0.finish_halves())
+    stores[4].start()
+    red_q[64:96] = sq2.finish()
+    red_q[32:64] = sq1.finish()
+    red_q[0:32] = sq0.finish()
+    stores[2].start()
+    red_n[...] = sn.finish()
+    stores[6].start()
     local = jnp.zeros((8, 128), F32)
     for ref in (red_q, red_o, red_u, red_d, red_n):
         local = local + jnp.sum(ref[...] * ref[...])
@@ -1018,27 +1062,37 @@
         return 0
 
     lax.fori_loop(1, 32, share_start, 0)
-    for part in (count_x, gro_x, gqkv_x, *scatters, scatter_p):
+    for part in (count_x, gro_x, *gqkv_x, *scatters):
         part.drain()
+    for copy in (mate_h, mate_g, mate_back, mate_y):
+        copy.wait_send()
     lax.fori_loop(1, 32, share_wait, 0)
     total[...] = jnp.sum(r.squares[...], axis=0)
+    stores[7].start()
+    for copy in stores:
+        copy.wait()
 
 
 def adam_kernel(*refs):
-    passed, state, outs = refs[0:2], refs[2:23], refs[23:46]
-    here, sems = refs[46:67], refs[67]
-    through = [pltpu.make_async_copy(a, b, sems.at[21 + k]) for k, (a, b) in enumerate(zip(passed, outs[21:23]))]
-    loads = [pltpu.make_async_copy(a, b, sems.at[k]) for k, (a, b) in enumerate(zip(state, here))]
-    for copy in (*loads, *through):
-        copy.start()
+    given, made, here, there, sems = refs[0:23], refs[23:46], refs[46:69], refs[69:90], refs[90]
+    loads = [pltpu.make_async_copy(a, b, sems.at[k]) for k, (a, b) in enumerate(zip(given, here))]
+    stores = [pltpu.make_async_copy(a, b, sems.at[23 + k]) for k, (a, b) in enumerate(zip((*there, *here[21:23]), made))]
+    order = (2, 3, 0, 1, 4)
+    loads[20].start()
+    for k in order:
+        for part in range(4):
+            loads[5 * part + k].start()
+    for k in (22, 21):
+        loads[k].start()
     fix_one = 1.0 - beta_one**STEP
     fix_two = 1.0 - beta_two**STEP
     rates = (rate_matrix, rate_output, rate_matrix, rate_matrix, rate_norm)
     loads[20].wait()
     norm = jnp.sqrt(here[20][0:1, 0:1])
     factor = 1.0 / jnp.maximum(norm, 1.0)
-    outs[20][...] = norm
-    for k in range(5):
+    there[20][...] = norm
+    stores[20].start()
+    for k in order:
         for part in range(4):
             loads[5 * part + k].wait()
         raw = here[k][...]
@@ -1052,11 +1106,17 @@
         second = beta_two * here[15 + k][...] + (1.0 - beta_two) * grad * grad
         stride = first / fix_one / (jnp.sqrt(second / fix_two) + adam_eps)
         decay = 0.0 if k == 4 else decay_rate
-        outs[k][...] = grad
-        outs[5 + k][...] = weight - rates[k] * (stride + decay * weight)
-        outs[10 + k][...] = first
-        outs[15 + k][...] = second
-    for copy in through:
+        there[k][...] = grad
+        there[5 + k][...] = weight - rates[k] * (stride + decay * weight)
+        there[10 + k][...] = first
+        there[15 + k][...] = second
+        for part in range(4):
+            stores[5 * part + k].start()
+        if k == 2:
+            for j in (22, 21):
+                loads[j].wait()
+                stores[j].start()
+    for copy in stores:
         copy.wait()
 
 
@@ -1064,16 +1124,15 @@
     layer_input, d_out, rand_ids, live_mask, w_qkv, w_out, w_up, w_down, norm_params,
     m_qkv, m_out, m_up, m_down, m_norm, v_qkv, v_out, v_up, v_down, v_norm,
 ):
-    vmem, smem, anywhere = (pl.BlockSpec(memory_space=kind) for kind in (pltpu.VMEM, pltpu.SMEM, pl.ANY))
+    smem, anywhere = (pl.BlockSpec(memory_space=kind) for kind in (pltpu.SMEM, pl.ANY))
     ids = rand_ids.transpose(0, 2, 3, 1).reshape(24, 6)
     leaves, tree = jax.tree.flatten(scratch())
-    reduced = [(96, 576), (48, 384), (96, 768), (192, 384), (8, 128), (8, 128)]
     shape = jax.ShapeDtypeStruct
     output, d_input, *grads, total = pl.pallas_call(
         functools.partial(kernel, tree),
-        out_shape=[shape((256, 768), BF16), shape((256, 768), F32)] + [shape(dims, F32) for dims in reduced],
-        in_specs=[smem, smem] + [vmem] * 7,
-        out_specs=[vmem] * 8,
+        out_shape=[shape(*leaf) for leaf in KEPT],
+        in_specs=[smem, smem] + [anywhere] * 7,
+        out_specs=[anywhere] * 8,
         scratch_shapes=leaves,
         compiler_params=pltpu.CompilerParams(collective_id=0, has_side_effects=True, vmem_limit_bytes=VMEM_LIMIT),
     )(
@@ -1085,17 +1144,18 @@
         w_qkv, w_out, w_up, w_down.T, norm_params.reshape(1, 96),
         m_qkv, m_out, m_up, m_down.T, m_norm.reshape(1, 96),
         v_qkv, v_out, v_up, v_down.T, v_norm.reshape(1, 96),
-        total,
-    )
+        total, output, d_input,
+    )
+    results = [shape(w.shape, F32) for w in state[5:10]] * 4
+    results += [shape((1, 1), F32), shape(output.shape, BF16), shape(d_input.shape, F32)]
     made = pl.pallas_call(
         adam_kernel,
-        out_shape=[shape(w.shape, F32) for w in state[5:10]] * 4
-        + [shape((1, 1), F32), shape(output.shape, BF16), shape(d_input.shape, F32)],
+        out_shape=results,
         in_specs=[anywhere] * 23,
-        out_specs=[vmem] * 23,
-        scratch_shapes=[pltpu.VMEM(a.shape, F32) for a in state] + [pltpu.SemaphoreType.DMA((23,))],
+        out_specs=[anywhere] * 23,
+        scratch_shapes=[pltpu.VMEM(a.shape, a.dtype) for a in (*state, *results[:21])] + [pltpu.SemaphoreType.DMA((46,))],
         compiler_params=pltpu.CompilerParams(vmem_limit_bytes=VMEM_LIMIT),
-    )(output, d_input, *state)
+    )(*state)
     updated = [m.T if k % 5 == 3 else m.reshape(-1) if k % 5 == 4 else m for k, m in enumerate(made[:20])]
     return (made[21].reshape(2, 128, 768), made[22].reshape(2, 128, 768), *updated, made[20].reshape(1))
 

time: 220 us -> 183 us (0.83)
  Pallas kernels: 217 us -> 181 us
    pallas_call x2, Pallas kernels: 217 us -> 181 us  [the longest x1 176 us: fused_device(): pl.pallas_call(functools.partial(kernel, tree), out_shape=[shape(*leaf) f...]
where the time goes in v3:
time: 183 us
  Pallas kernels  181 us (99%)
    pallas_call x1, Pallas kernels, fused_device(): pl.pallas_call(functools.partial(kernel, tree), out_shape=[shape(*leaf) f...  176 us
    pallas_call x1, Pallas kernels, fused_device(): pl.pallas_call(adam_kernel, out_shape=results, in_specs=[anywhere] * 23,...  4.72 us

profile of v3, /device:TPU:0, one launch (start us, length us, event | category | flops | bytes accessed | tf_op | source)
XLA Modules:
  0.0 183.0 jit_solution(14364445624659023777)
XLA Ops:
  0.7 0.0 copy-start
  0.7 0.7 copy-done
  1.4 0.1 reshape.86
  1.4 0.7 copy.44.rand_ids
  2.1 176.0 %shard_map.362 = (bf16[256,768]{1,0:T(8,128)(2,1)}, f32[256,768]{1,0:T(8,128)}, f32[96,576]{1,0:T(8,128)}, f32[48,384]{1,0:T(8,128)}, f32[96,768]{1,0:T(8,128)},...) custom-call(s32[2]{0:T(128)} %live.1, s32[24,6]{1,0:T(8,128)} %copy.44.rand_ids, ...), custom_call_target="tpu_custom_call" | custom-call | tf_op jit(solution)/shard_map/pallas_call | solution.py:1131
  178.1 4.7 %shard_map.363 = (f32[96,576]{1,0:T(8,128)}, f32[96,192]{1,0:T(8,128)}, f32[96,768]{1,0:T(8,128)}, f32[192,384]{1,0:T(8,128)}, f32[1,96]{1,0:T(1,128)}, /*index=...) custom-call(f32[96,576]{1,0:T(8,128)} %get-tuple-element.54.refs_0_,, ...), custom_call_target="tpu_custom_call" | custom-call | tf_op jit(solution)/shard_map/pallas_call | solution.py:1151
  (1 shorter events, 0.0 us)
Async XLA Ops:
  0.7 0.7 copy-start
